TPU v7x, 32 devices: a whole 2x2x4 slice. The times are simulated.
32 devices in a mesh: lon: 8 (over y, x, core), lat: 4 (over z).
Axes of the slice: x: 2, y: 2, z: 4, core: 2. Of those that a mesh axis runs over, the one named last changes fastest.
Arguments:
- fields: float32 [5, 1, 128, 11520], P(None, None, 'lat', 'lon'), may hold values from -6 to 6
- frac_x: float32 [2, 1, 128], replicated, may hold values from 0.05 to 0.95
- frac_y: float32 [2, 1, 128], replicated, may hold values from 0.05 to 0.9
- shift_cells: int32 [2, 1, 128], replicated, may hold values from -5760 to 5759, as said below
- polar_mask: int32 [128], replicated, may hold values from 0 to 1, as said below
Outputs:
- fields_out: float32 [5, 1, 128, 11520], P(None, None, 'lat', 'lon')
Inputs may be any that keep to these rules, and one draw needn't show every extreme that they name: `shift_cells`: outside the first and last 32 rows every count lies in -2 .. 1, and both -2 and 1 occur there. `polar_mask`: nonzero only in the first and last 32 rows; the first and the last row are 1.
All inputs are finite; a program needn't handle non-finite values.
Results may differ from a plain program's by a relative error of at most 0.00016.
Values sent between devices are 32-bit elements; how exact they have to be, the bound alone decides.
A program may use at most 64 MiB of HBM per device.

v0:
```python
import math

import jax
import jax.numpy as jnp
from jax import lax
from jax.sharding import PartitionSpec as P

FA = 90
FB = 128
SUBS = 2
REACH = 4


def passed_along(x, axis, by):
    devices = lax.axis_size(axis)
    return lax.ppermute(x, axis, [(i, (i + by) % devices) for i in range(devices)])


def passed_along_2(block, axis, distance):
    devices = range(lax.axis_size(axis))
    route = [(i - distance, i) for i in devices if i - distance in devices]
    return lax.ppermute(block, axis, route)


def roll_digits(values, amount, span, axis):
    bit_total = max((span - 1).bit_length(), 1)
    for bit in range(bit_total):
        moved = jnp.roll(values, 1 << bit, axis=axis)
        taken = amount >> bit & 1 == 1
        values = jnp.where(taken, moved, values)
    return values


def cycle_move(state, counts, lon_cells):
    device_jump = jnp.floor_divide(counts, lon_cells)
    remainder = counts - device_jump * lon_cells
    select = device_jump + REACH
    bit_count = (2 * REACH).bit_length() - 1
    offsets = [-REACH] + [1 << bit for bit in range(bit_count)]
    current = state
    for turn, offset in enumerate(offsets):
        moved = passed_along(current, "lon", offset)
        if turn == 0:
            current = moved
        else:
            taken = select >> turn - 1 & 1 == 1
            current = jnp.where(taken[None, :, :, None], moved, current)
    western = passed_along(current, "lon", 1)
    joined = jnp.concatenate([western, current], axis=3)
    rolled = roll_digits(joined, remainder[None, :, :, None], lon_cells, 3)
    return rolled[:, :, :, lon_cells:]


def zonal_fraction(whole, courant):
    previous = jnp.roll(whole, 1, axis=1)
    edge = whole + 0.5 * (1.0 - courant) * (whole - previous)
    return whole - courant * (edge - jnp.roll(edge, 1, axis=1))


def polar_smooth(whole, lat_rows, marks, lat_cells, lat_total):
    row_count, lon_total = whole.shape
    highest = lax.Precision.HIGHEST
    first_ids = jnp.arange(FA, dtype=jnp.int32)
    second_ids = jnp.arange(FB, dtype=jnp.int32)
    angle_first = (
        2.0 * math.pi * (first_ids[:, None] * first_ids[None, :] % FA).astype(jnp.float32) / FA
    )
    cos_first, sin_first = (jnp.cos(angle_first), jnp.sin(angle_first))
    angle_second = (
        2.0 * math.pi * (second_ids[:, None] * second_ids[None, :] % FB).astype(jnp.float32) / FB
    )
    cos_second, sin_second = (jnp.cos(angle_second), jnp.sin(angle_second))
    angle_twist = (
        2.0
        * math.pi
        * (first_ids[:, None] * second_ids[None, :] % lon_total).astype(jnp.float32)
        / lon_total
    )
    cos_twist, sin_twist = (jnp.cos(angle_twist), jnp.sin(angle_twist))
    waves = (first_ids[:, None] + FA * second_ids[None, :]).astype(jnp.float32)
    sine = jnp.sin(math.pi * waves / lon_total)
    phi = math.pi * (lat_rows.astype(jnp.float32) + 0.5) / lat_total - math.pi / 2
    edge_cos = math.sin(math.pi * (lat_cells - 0.5) / lat_total)
    b_val = jnp.cos(phi) / edge_cos
    gain = 1.0 / (1.0 + sine[None, :, :] ** 2 / b_val[:, None, None] ** 2)
    grid = whole.reshape(row_count, FA, FB)
    real_one = jnp.einsum("kn,rnm->rkm", cos_first, grid, precision=highest)
    imag_one = -jnp.einsum("kn,rnm->rkm", sin_first, grid, precision=highest)
    real_two = real_one * cos_twist + imag_one * sin_twist
    imag_two = imag_one * cos_twist - real_one * sin_twist
    real_spec = jnp.einsum("rkm,mq->rkq", real_two, cos_second, precision=highest) + jnp.einsum(
        "rkm,mq->rkq", imag_two, sin_second, precision=highest
    )
    imag_spec = jnp.einsum("rkm,mq->rkq", imag_two, cos_second, precision=highest) - jnp.einsum(
        "rkm,mq->rkq", real_two, sin_second, precision=highest
    )
    real_spec = real_spec * gain
    imag_spec = imag_spec * gain
    real_back = jnp.einsum("rkq,mq->rkm", real_spec, cos_second, precision=highest) - jnp.einsum(
        "rkq,mq->rkm", imag_spec, sin_second, precision=highest
    )
    imag_back = jnp.einsum("rkq,mq->rkm", imag_spec, cos_second, precision=highest) + jnp.einsum(
        "rkq,mq->rkm", real_spec, sin_second, precision=highest
    )
    real_turn = real_back * cos_twist - imag_back * sin_twist
    imag_turn = imag_back * cos_twist + real_back * sin_twist
    result = jnp.einsum("kn,rkm->rnm", cos_first, real_turn, precision=highest) - jnp.einsum(
        "kn,rkm->rnm", sin_first, imag_turn, precision=highest
    )
    result = result.reshape(row_count, lon_total) / lon_total
    return jnp.where((marks == 1)[:, None], result, whole)


def meridional(state, merid_step, first_row):
    n_fields, n_levels, lat_cells, lon_cells = state.shape
    southern = passed_along_2(state[:, :, lat_cells - 2 :, :], "lat", 1)
    extended = jnp.concatenate([southern, state], axis=2)
    padded_faces = jnp.concatenate([merid_step, jnp.zeros((n_levels, 1), jnp.float32)], axis=1)
    faces = lax.dynamic_slice_in_dim(padded_faces, first_row, lat_cells + 1, 1)
    face_ids = first_row + jnp.arange(lat_cells + 1, dtype=jnp.int32)
    faces = jnp.where((face_ids == 0)[None, :], jnp.zeros_like(faces), faces)
    courant = faces[None, :, :, None]
    upper = extended[:, :, 1 : lat_cells + 2, :]
    lower = extended[:, :, 0 : lat_cells + 1, :]
    flux = courant * (upper + 0.5 * (1.0 - courant) * (upper - lower))
    return state + flux[:, :, :lat_cells, :] - flux[:, :, 1:, :]


def body(fields, frac_x, frac_y, shift_cells, polar_mask):
    n_fields, n_levels, lat_cells, lon_cells = fields.shape
    lon_devs = lax.axis_size("lon")
    lat_total = lat_cells * lax.axis_size("lat")
    lon_index = lax.axis_index("lon")
    first_row = lax.axis_index("lat") * lat_cells
    row_total = n_fields * n_levels * lat_cells
    per_device = row_total // lon_devs
    row_start = lon_index * per_device
    local_rows = first_row + jnp.arange(lat_cells, dtype=jnp.int32)
    marks_local = lax.dynamic_slice_in_dim(polar_mask, first_row, lat_cells, 0)

    def my_rows(table):
        spread = jnp.broadcast_to(table[None], (n_fields, n_levels, lat_cells)).reshape(row_total)
        return lax.dynamic_slice_in_dim(spread, row_start, per_device, 0)

    row_lats = my_rows(local_rows[None])
    row_marks = my_rows(marks_local[None])
    state = fields
    for substep in range(SUBS):
        counts = lax.dynamic_slice_in_dim(shift_cells[substep], first_row, lat_cells, 1)
        fractions = lax.dynamic_slice_in_dim(frac_x[substep], first_row, lat_cells, 1)
        placed = cycle_move(state, counts, lon_cells)
        flat = placed.reshape(row_total, lon_cells)
        whole = lax.all_to_all(flat, "lon", split_axis=0, concat_axis=1, tiled=True)
        whole = zonal_fraction(whole, my_rows(fractions)[:, None])
        whole = polar_smooth(whole, row_lats, row_marks, lat_cells, lat_total)
        blocks = lax.all_to_all(whole, "lon", split_axis=1, concat_axis=0, tiled=True)
        state = blocks.reshape(n_fields, n_levels, lat_cells, lon_cells)
        state = meridional(state, frac_y[substep], first_row)
    return state


def solution(mesh):
    return jax.shard_map(
        body,
        mesh=mesh,
        in_specs=(P(None, None, "lat", "lon"), P(), P(), P(), P()),
        out_specs=P(None, None, "lat", "lon"),
        check_vma=False,
    )
```

profile of v0, /device:TPU:0, one launch (start us, length us, event | category | flops | bytes accessed | tf_op | source)
XLA Modules:
  0.0 374.6 jit_solution(14722888508883360047)
XLA Ops:
  0.0 3.0 collective-permute-start
  3.0 22.0 %collective-permute-done = f32[5,1,32,1440]{3,2,1,0:T(8,128)S(1)} collective-permute-done((f32[5,1,32,1440]{3,2,1,0:T(8,128)}, f32[5,1,32,1440]{3,2,1,0:T(8,128)S(1)}, u32[]{:S(2)}, u32[]{:S(2)}) %collective-permute-start) | collective-permute-done | bytes 921632 | tf_op jit(solution)/shard_map/ppermute | solution.py:16
  26.3 13.1 %collective-permute-done.1 = f32[5,1,32,1440]{3,2,1,0:T(8,128)S(1)} collective-permute-done((f32[5,1,32,1440]{3,2,1,0:T(8,128)S(1)}, f32[5,1,32,1440]{3,2,1,0:T(8,128)S(1)}, u32[]{:S(2)}, u32[]{:S(2)}) %collective-permute-start.1) | collective-permute-done | bytes 921632 | tf_op jit(solution)/shard_map/ppermute | solution.py:16
  40.4 22.2 %collective-permute-done.2 = f32[5,1,32,1440]{3,2,1,0:T(8,128)S(1)} collective-permute-done((f32[5,1,32,1440]{3,2,1,0:T(8,128)S(1)}, f32[5,1,32,1440]{3,2,1,0:T(8,128)S(1)}, u32[]{:S(2)}, u32[]{:S(2)}) %collective-permute-start.2) | collective-permute-done | bytes 921632 | tf_op jit(solution)/shard_map/ppermute | solution.py:16
  62.8 1.6 collective-permute-start.3
  64.4 19.7 %collective-permute-done.3 = f32[5,1,32,1440]{3,2,1,0:T(8,128)S(1)} collective-permute-done((f32[5,1,32,1440]{3,2,1,0:T(8,128)S(1)}, f32[5,1,32,1440]{3,2,1,0:T(8,128)S(1)}, u32[]{:S(2)}, u32[]{:S(2)}) %collective-permute-start.3) | collective-permute-done | bytes 921632 | tf_op jit(solution)/shard_map/ppermute | solution.py:16
  85.2 13.6 %collective-permute-done.4 = f32[5,1,32,1440]{3,2,1,0:T(8,128)S(1)} collective-permute-done((f32[5,1,32,1440]{3,2,1,0:T(8,128)S(1)}, f32[5,1,32,1440]{3,2,1,0:T(8,128)S(1)}, u32[]{:S(2)}, u32[]{:S(2)}) %collective-permute-start.4) | collective-permute-done | bytes 921632 | tf_op jit(solution)/shard_map/ppermute | solution.py:16
  107.5 3.8 %all-to-all-start = ((f32[8,20,1440]{2,1,0:T(8,128)}), f32[8,20,1440]{2,1,0:T(8,128)S(1)}, u32[]{:S(2)}, u32[]{:S(2)}) async-start(f32[8,20,1440]{2,1,0:T(8,128)} %all_to_all.52), calls=%async_computation | async-start | bytes 2359296 | tf_op jit(solution)/shard_map/all_to_all | solution.py:153
  112.8 15.0 %all-to-all-done = f32[8,20,1440]{2,1,0:T(8,128)S(1)} async-done(((f32[8,20,1440]{2,1,0:T(8,128)}), f32[8,20,1440]{2,1,0:T(8,128)S(1)}, u32[]{:S(2)}, u32[]{:S(2)}) %all-to-all-start) | async-done | bytes 921632 | tf_op jit(solution)/shard_map/all_to_all | solution.py:153
  128.4 1.4 all_to_all.55
  131.2 1.6 concatenate.853
  134.1 1.6 concatenate.852
  136.8 2.1 multiply_subtract_fusion.3
  138.9 1.2 fusion.13
  140.1 1.2 convolution_bitcast_fusion.1
  143.7 1.2 fusion.11
  144.9 1.6 fusion.75
  146.5 1.2 fusion.12
  151.2 1.3 fusion.42
  152.5 2.3 fusion.10
  154.8 2.9 div.293
  157.7 4.0 %copy_select_fusion.1 = f32[20,8,1440]{2,0,1:T(8,128)} fusion(f32[20,8,1440]{2,1,0:T(8,128)} %div.293, f32[20,8,1440]{2,1,0:T(8,128)S(1)} %copy-done.2, f32[20,8,1440]{2,1,0:T(8,128)S(1)} %copy-done.3, f32[20]{0:T(128)S(1)} %get-tuple-element.18, f32[20]{0:T(128)S(1)} %get-tuple-element.19, pred[20]{0:T(512)(128)(4,1)S(1)} %dynamic-slice_compare_fusion, ...), kind=kLoop, calls=%fused_computation.69 | loop fusion | flops 1612800 | bytes 4608180 | tf_op jit(solution)/shard_map/jit(_where)/select_n | solution.py:111
  161.7 3.7 all-to-all-start.1
  166.0 16.2 %all-to-all-done.1 = f32[20,8,1440]{2,0,1:T(8,128)S(1)} async-done(((f32[20,8,1440]{2,0,1:T(8,128)}), f32[20,8,1440]{2,0,1:T(8,128)S(1)}, u32[]{:S(2)}, u32[]{:S(2)}) %all-to-all-start.1) | async-done | bytes 921632 | tf_op jit(solution)/shard_map/all_to_all | solution.py:156
  182.3 3.3 collective-permute-start.5
  185.6 1.8 collective-permute-done.5
  188.6 19.2 %collective-permute-done.6 = f32[5,1,32,1440]{3,2,0,1:T(8,128)S(1)} collective-permute-done((f32[5,1,32,1440]{3,2,0,1:T(8,128)S(1)}, f32[5,1,32,1440]{3,2,0,1:T(8,128)S(1)}, u32[]{:S(2)}, u32[]{:S(2)}) %collective-permute-start.6) | collective-permute-done | bytes 921632 | tf_op jit(solution)/shard_map/ppermute | solution.py:16
  207.9 14.4 %collective-permute-done.7 = f32[5,1,32,1440]{3,2,0,1:T(8,128)S(1)} collective-permute-done((f32[5,1,32,1440]{3,2,0,1:T(8,128)S(1)}, f32[5,1,32,1440]{3,2,0,1:T(8,128)S(1)}, u32[]{:S(2)}, u32[]{:S(2)}) %collective-permute-start.7) | collective-permute-done | bytes 921632 | tf_op jit(solution)/shard_map/ppermute | solution.py:16
  222.5 2.9 collective-permute-start.8
  225.4 22.2 %collective-permute-done.8 = f32[5,1,32,1440]{3,2,0,1:T(8,128)S(1)} collective-permute-done((f32[5,1,32,1440]{3,2,0,1:T(8,128)S(1)}, f32[5,1,32,1440]{3,2,0,1:T(8,128)S(1)}, u32[]{:S(2)}, u32[]{:S(2)}) %collective-permute-start.8) | collective-permute-done | bytes 921632 | tf_op jit(solution)/shard_map/ppermute | solution.py:16
  248.2 22.8 %collective-permute-done.9 = f32[5,1,32,1440]{3,2,0,1:T(8,128)S(1)} collective-permute-done((f32[5,1,32,1440]{3,2,0,1:T(8,128)S(1)}, f32[5,1,32,1440]{3,2,0,1:T(8,128)S(1)}, u32[]{:S(2)}, u32[]{:S(2)}) %collective-permute-start.9) | collective-permute-done | bytes 921632 | tf_op jit(solution)/shard_map/ppermute | solution.py:16
  271.4 14.3 %collective-permute-done.10 = f32[5,1,32,1440]{3,2,0,1:T(8,128)S(1)} collective-permute-done((f32[5,1,32,1440]{3,2,0,1:T(8,128)S(1)}, f32[5,1,32,1440]{3,2,0,1:T(8,128)S(1)}, u32[]{:S(2)}, u32[]{:S(2)}) %collective-permute-start.10) | collective-permute-done | bytes 921632 | tf_op jit(solution)/shard_map/ppermute | solution.py:16
  294.5 3.8 %all-to-all-start.2 = ((f32[8,20,1440]{2,1,0:T(8,128)}), f32[8,20,1440]{2,1,0:T(8,128)S(1)}, u32[]{:S(2)}, u32[]{:S(2)}) async-start(f32[8,20,1440]{2,1,0:T(8,128)} %all_to_all.59), calls=%async_computation.2 | async-start | bytes 2359296 | tf_op jit(solution)/shard_map/all_to_all | solution.py:153
  298.4 16.3 %all-to-all-done.2 = f32[8,20,1440]{2,1,0:T(8,128)S(1)} async-done(((f32[8,20,1440]{2,1,0:T(8,128)}), f32[8,20,1440]{2,1,0:T(8,128)S(1)}, u32[]{:S(2)}, u32[]{:S(2)}) %all-to-all-start.2) | async-done | bytes 921632 | tf_op jit(solution)/shard_map/all_to_all | solution.py:153
  315.3 1.4 all_to_all.62
  318.2 1.6 concatenate.873
  321.0 1.6 concatenate.872
  323.8 2.1 multiply_subtract_fusion.1
  325.9 1.2 fusion.8
  330.6 1.2 fusion.6
  333.0 1.4 fusion.7
  338.0 1.3 fusion.35
  339.3 2.3 fusion.5
  341.6 2.9 div.296
  344.5 2.9 copy_select_fusion
  347.5 19.2 %all_to_all.70 = f32[20,8,1440]{2,0,1:T(8,128)S(1)} all-to-all(f32[20,8,1440]{2,0,1:T(8,128)S(1)} %copy_select_fusion), channel_id=1, replica_groups=mesh['lon'=8,'lat'=4] {'lon'}, dimensions={1} | all-to-all | bytes 1843200 | tf_op jit(solution)/shard_map/all_to_all | solution.py:156
  366.8 4.0 %collective-permute-start.11 = (f32[5,1,2,1440]{3,2,0,1:T(2,128)S(1)}, f32[5,1,2,1440]{3,2,0,1:T(2,128)S(1)}, u32[]{:S(2)}, u32[]{:S(2)}) collective-permute-start(f32[5,1,2,1440]{3,2,0,1:T(2,128)S(1)} %slice.367), channel_id=1, source_target_pairs={{0,1},{1,2},{2,3},{4,5},{5,6},{6,7},{8,9},{9,10},{10,11},{12,13},{... | collective-permute-start | bytes 172808 | tf_op jit(solution)/shard_map/ppermute | solution.py:22
  370.8 1.8 collective-permute-done.11
  (164 shorter events, 50.0 us)
Async XLA Ops:
  0.0 24.9 %collective-permute-start = (f32[5,1,32,1440]{3,2,1,0:T(8,128)}, f32[5,1,32,1440]{3,2,1,0:T(8,128)S(1)}, u32[]{:S(2)}, u32[]{:S(2)}) collective-permute-start(f32[5,1,32,1440]{3,2,1,0:T(8,128)} %param.5), channel_id=1, source_target_pairs={{0,16},{4,20},{8,24},{12,28},{16,0},{20,4},{24,8},{28,12},{1,17},{... | collective-permute-start | bytes 2764808 | tf_op jit(solution)/shard_map/ppermute | solution.py:16
  24.9 14.4 %collective-permute-start.1 = (f32[5,1,32,1440]{3,2,1,0:T(8,128)S(1)}, f32[5,1,32,1440]{3,2,1,0:T(8,128)S(1)}, u32[]{:S(2)}, u32[]{:S(2)}) collective-permute-start(f32[5,1,32,1440]{3,2,1,0:T(8,128)S(1)} %collective-permute-done), channel_id=1, source_target_pairs={{0,4},{4,8},{8,12},{12,16},{16,20},{20,24},{24,28},{28,0},{1,5},{5... | collective-permute-start | bytes 2764808 | tf_op jit(solution)/shard_map/ppermute | solution.py:16
  39.6 23.1 %collective-permute-start.2 = (f32[5,1,32,1440]{3,2,1,0:T(8,128)S(1)}, f32[5,1,32,1440]{3,2,1,0:T(8,128)S(1)}, u32[]{:S(2)}, u32[]{:S(2)}) collective-permute-start(f32[5,1,32,1440]{3,2,1,0:T(8,128)S(1)} %broadcast_select_fusion), channel_id=1, source_target_pairs={{0,8},{4,12},{8,16},{12,20},{16,24},{20,28},{24,0},{28,4},{1,9},{5... | collective-permute-start | bytes 2764808 | tf_op jit(solution)/shard_map/ppermute | solution.py:16
  62.8 21.5 %copy-start.12 = (s32[128]{0:T(128)S(1)}, s32[128]{0:T(128)}, u32[]{:S(2)}) copy-start(s32[128]{0:T(128)} %param.9) | copy-start | bytes 1540
  62.8 21.6 %copy-start.10 = (f32[2,1,128]{2,1,0:T(1,128)S(1)}, f32[2,1,128]{2,1,0:T(1,128)}, u32[]{:S(2)}) copy-start(f32[2,1,128]{2,1,0:T(1,128)} %param.6) | copy-start | bytes 3076
  62.8 21.3 %collective-permute-start.3 = (f32[5,1,32,1440]{3,2,1,0:T(8,128)S(1)}, f32[5,1,32,1440]{3,2,1,0:T(8,128)S(1)}, u32[]{:S(2)}, u32[]{:S(2)}) collective-permute-start(f32[5,1,32,1440]{3,2,1,0:T(8,128)S(1)} %broadcast_select_fusion.1), channel_id=1, source_target_pairs={{0,16},{4,20},{8,24},{12,28},{16,0},{20,4},{24,8},{28,12},{1,17},{... | collective-permute-start | bytes 2764808 | tf_op jit(solution)/shard_map/ppermute | solution.py:16
  84.3 14.5 %collective-permute-start.4 = (f32[5,1,32,1440]{3,2,1,0:T(8,128)S(1)}, f32[5,1,32,1440]{3,2,1,0:T(8,128)S(1)}, u32[]{:S(2)}, u32[]{:S(2)}) collective-permute-start(f32[5,1,32,1440]{3,2,1,0:T(8,128)S(1)} %broadcast_select_fusion.2), channel_id=1, source_target_pairs={{0,4},{4,8},{8,12},{12,16},{16,20},{20,24},{24,28},{28,0},{1,5},{5... | collective-permute-start | bytes 2764808 | tf_op jit(solution)/shard_map/ppermute | solution.py:16
  107.5 20.3 %all-to-all-start = ((f32[8,20,1440]{2,1,0:T(8,128)}), f32[8,20,1440]{2,1,0:T(8,128)S(1)}, u32[]{:S(2)}, u32[]{:S(2)}) async-start(f32[8,20,1440]{2,1,0:T(8,128)} %all_to_all.52), calls=%async_computation | async-start | bytes 2359296 | tf_op jit(solution)/shard_map/all_to_all | solution.py:153
  134.0 2.8 copy-start.4
  142.4 1.2 copy-start.13
  154.8 2.9 copy-start.2
  154.8 2.9 copy-start.3
  161.7 3.7 copy-start.11
  161.7 20.4 %all-to-all-start.1 = ((f32[20,8,1440]{2,0,1:T(8,128)}), f32[20,8,1440]{2,0,1:T(8,128)S(1)}, u32[]{:S(2)}, u32[]{:S(2)}) async-start(f32[20,8,1440]{2,0,1:T(8,128)} %copy_select_fusion.1), calls=%async_computation.1 | async-start | bytes 2359296 | tf_op jit(solution)/shard_map/all_to_all | solution.py:156
  182.3 5.1 %collective-permute-start.5 = (f32[5,1,2,1440]{3,2,0,1:T(2,128)S(1)}, f32[5,1,2,1440]{3,2,0,1:T(2,128)S(1)}, u32[]{:S(2)}, u32[]{:S(2)}) collective-permute-start(f32[5,1,2,1440]{3,2,0,1:T(2,128)S(1)} %slice.334), channel_id=1, source_target_pairs={{0,1},{1,2},{2,3},{4,5},{5,6},{6,7},{8,9},{9,10},{10,11},{12,13},{... | collective-permute-start | bytes 172808 | tf_op jit(solution)/shard_map/ppermute | solution.py:22
  187.8 20.1 %copy-start.7 = (s32[32]{0:T(128)S(1)}, s32[32]{0:T(128)}, u32[]{:S(2)}) copy-start(s32[32]{0:T(128)} %get-tuple-element.57) | copy-start | bytes 388
  188.0 19.8 %collective-permute-start.6 = (f32[5,1,32,1440]{3,2,0,1:T(8,128)S(1)}, f32[5,1,32,1440]{3,2,0,1:T(8,128)S(1)}, u32[]{:S(2)}, u32[]{:S(2)}) collective-permute-start(f32[5,1,32,1440]{3,2,0,1:T(8,128)S(1)} %slice_subtract_fusion.1), channel_id=1, source_target_pairs={{0,16},{4,20},{8,24},{12,28},{16,0},{20,4},{24,8},{28,12},{1,17},{... | collective-permute-start | bytes 2764808 | tf_op jit(solution)/shard_map/ppermute | solution.py:16
  207.9 14.4 %collective-permute-start.7 = (f32[5,1,32,1440]{3,2,0,1:T(8,128)S(1)}, f32[5,1,32,1440]{3,2,0,1:T(8,128)S(1)}, u32[]{:S(2)}, u32[]{:S(2)}) collective-permute-start(f32[5,1,32,1440]{3,2,0,1:T(8,128)S(1)} %collective-permute-done.6), channel_id=1, source_target_pairs={{0,4},{4,8},{8,12},{12,16},{16,20},{20,24},{24,28},{28,0},{1,5},{5... | collective-permute-start | bytes 2764808 | tf_op jit(solution)/shard_map/ppermute | solution.py:16
  222.5 25.1 %collective-permute-start.8 = (f32[5,1,32,1440]{3,2,0,1:T(8,128)S(1)}, f32[5,1,32,1440]{3,2,0,1:T(8,128)S(1)}, u32[]{:S(2)}, u32[]{:S(2)}) collective-permute-start(f32[5,1,32,1440]{3,2,0,1:T(8,128)S(1)} %broadcast_select_fusion.3), channel_id=1, source_target_pairs={{0,8},{4,12},{8,16},{12,20},{16,24},{20,28},{24,0},{28,4},{1,9},{5... | collective-permute-start | bytes 2764808 | tf_op jit(solution)/shard_map/ppermute | solution.py:16
  247.8 23.5 %copy-start.8 = (s32[32]{0:T(128)S(1)}, s32[32]{0:T(128)}, u32[]{:S(2)}) copy-start(s32[32]{0:T(128)} %get-tuple-element.56) | copy-start | bytes 388
  247.8 23.3 %collective-permute-start.9 = (f32[5,1,32,1440]{3,2,0,1:T(8,128)S(1)}, f32[5,1,32,1440]{3,2,0,1:T(8,128)S(1)}, u32[]{:S(2)}, u32[]{:S(2)}) collective-permute-start(f32[5,1,32,1440]{3,2,0,1:T(8,128)S(1)} %broadcast_select_fusion.4), channel_id=1, source_target_pairs={{0,16},{4,20},{8,24},{12,28},{16,0},{20,4},{24,8},{28,12},{1,17},{... | collective-permute-start | bytes 2764808 | tf_op jit(solution)/shard_map/ppermute | solution.py:16
  271.3 14.5 %collective-permute-start.10 = (f32[5,1,32,1440]{3,2,0,1:T(8,128)S(1)}, f32[5,1,32,1440]{3,2,0,1:T(8,128)S(1)}, u32[]{:S(2)}, u32[]{:S(2)}) collective-permute-start(f32[5,1,32,1440]{3,2,0,1:T(8,128)S(1)} %broadcast_select_fusion.5), channel_id=1, source_target_pairs={{0,4},{4,8},{8,12},{12,16},{16,20},{20,24},{24,28},{28,0},{1,5},{5... | collective-permute-start | bytes 2764808 | tf_op jit(solution)/shard_map/ppermute | solution.py:16
  293.3 5.0 %copy-start.6 = (f32[32]{0:T(128)S(1)}, f32[32]{0:T(128)}, u32[]{:S(2)}) copy-start(f32[32]{0:T(128)} %get-tuple-element.61) | copy-start | bytes 388
  294.5 20.3 %all-to-all-start.2 = ((f32[8,20,1440]{2,1,0:T(8,128)}), f32[8,20,1440]{2,1,0:T(8,128)S(1)}, u32[]{:S(2)}, u32[]{:S(2)}) async-start(f32[8,20,1440]{2,1,0:T(8,128)} %all_to_all.59), calls=%async_computation.2 | async-start | bytes 2359296 | tf_op jit(solution)/shard_map/all_to_all | solution.py:153
  321.0 2.8 copy-start.5
  329.4 1.2 copy-start.14
  341.6 2.9 copy-start
  341.6 2.9 copy-start.1
  347.4 23.3 %copy-start.9 = (f32[1,128]{1,0:T(1,128)S(1)}, f32[1,128]{1,0:T(1,128)}, u32[]{:S(2)}) copy-start(f32[1,128]{1,0:T(1,128)} %get-tuple-element.23) | copy-start | bytes 1540
  366.8 5.8 %collective-permute-start.11 = (f32[5,1,2,1440]{3,2,0,1:T(2,128)S(1)}, f32[5,1,2,1440]{3,2,0,1:T(2,128)S(1)}, u32[]{:S(2)}, u32[]{:S(2)}) collective-permute-start(f32[5,1,2,1440]{3,2,0,1:T(2,128)S(1)} %slice.367), channel_id=1, source_target_pairs={{0,1},{1,2},{2,3},{4,5},{5,6},{6,7},{8,9},{9,10},{10,11},{12,13},{... | collective-permute-start | bytes 172808 | tf_op jit(solution)/shard_map/ppermute | solution.py:22
where the time goes:
time: 381 us; the launch traced here: 375 us
  waiting for transfers between devices  234 us (61%)
  matrix products  31.4 us (8%)
  local copies, waits for them, and re-layouts  30.5 us (8%)
  other arithmetic  29.7 us (8%)
  starting transfers between devices  27.9 us (7%)
  blocking collectives  19.2 us (5%)
    ppermute x10, waiting for transfers between devices, passed_along(): lax.ppermute(x, axis, [(i, (i + by) % devices) for i in range(devices)])  183 us
    all_to_all x2, waiting for transfers between devices, body(): whole = lax.all_to_all(flat, 'lon', split_axis=0, concat_axis=1, tiled=True)  31.3 us
    all_to_all x1, blocking collectives, body(): lax.all_to_all(whole, 'lon', split_axis=1, concat_axis=0, tiled=True)  19.2 us
    all_to_all x1, waiting for transfers between devices, body(): lax.all_to_all(whole, 'lon', split_axis=1, concat_axis=0, tiled=True)  16.2 us
    select_n x22, other arithmetic, roll_digits(): values = jnp.where(taken, moved, values)  11.1 us
    ppermute x10, starting transfers between devices, passed_along(): lax.ppermute(x, axis, [(i, (i + by) % devices) for i in range(devices)])  9.47 us
  transfers between devices with their start and end apart: 15, of which 15 were waited for; matrix products, arithmetic and copies ran while one was open for 1% of the time, Pallas kernels for 0%

commit v1 on v0

v1 whole, which is shorter than its diff:
```python
import functools
import math

import jax
import jax.numpy as jnp
import numpy as np
from jax import lax
from jax.experimental import pallas as pl
from jax.experimental.pallas import tpu as pltpu
from jax.sharding import PartitionSpec as P

SUBS = 2
LANES = 128
HALO = 2
MESH = pl.DeviceIdType.MESH
VMEM_LIMIT = 48 * 1024 * 1024


class Plan:
    def __init__(self, mesh, fields_shape):
        self.blocks = mesh.shape["lon"]
        self.bands = mesh.shape["lat"]
        self.fields, _, self.lat_total, self.lon_total = fields_shape
        self.lat = self.lat_total // self.bands
        self.lon = self.lon_total // self.blocks
        self.cols = -(-self.lon // LANES)
        self.rem = self.lon - LANES * (self.cols - 1)
        self.rows = self.fields * self.lat
        self.own = self.rows // self.blocks
        pitch = self.cols
        while (self.own * pitch) % 8 or (HALO * pitch) % 8:
            pitch += 1
        self.pitch = pitch
        self.slots = self.own + 2 * HALO
        self.unit = 2 if self.own % 2 == 0 else 1
        assert self.rows % self.blocks == 0 and self.own <= self.lat
        assert self.blocks & (self.blocks - 1) == 0 and self.blocks % 8 == 0 and self.lat % 8 == 0
        self.south_to = [
            (f, d)
            for f in range(self.fields)
            for d in sorted({f * self.lat // self.own, (f * self.lat + 1) // self.own})
        ]


def decay_table(plan):
    rows = np.arange(plan.lat_total, dtype=np.float64)
    phi = math.pi * (rows + 0.5) / plan.lat_total - math.pi / 2
    b = np.cos(phi) / math.sin(math.pi * (plan.lat - 0.5) / plan.lat_total)
    log_r = -2.0 * np.arcsinh(b)
    r = np.exp(log_r)
    lines = [np.exp(log_r * 2**k) for k in range(7)]
    lines += [np.exp(log_r * LANES), np.exp(log_r * plan.rem)]
    lines += [(1 - r) / (1 + r), 1 / (1 - np.exp(log_r * plan.lon_total)), log_r]
    lines += [np.exp(log_r * plan.lon * 2**k) for k in range(plan.blocks.bit_length() - 1)]
    table = np.stack(lines).astype(np.float32)
    return np.where(np.abs(table) < 1.2e-38, np.float32(0), table)


def spread_kernel(plan, x_ref, out_ref, packed, send, recv, south_send, south_recv, own_sem):
    me = lax.axis_index("lon")
    band = lax.axis_index("lat")
    blocks, pitch, own = plan.blocks, plan.pitch, plan.own
    packed[0 : HALO * pitch, :] = jnp.zeros((HALO * pitch, LANES), jnp.float32)

    def fill(group, carry):
        for c in range(plan.cols):
            width = LANES if c < plan.cols - 1 else plan.rem
            v = x_ref[pl.ds(pl.multiple_of(group * 8, 8), 8), c * LANES : c * LANES + width]
            if width < LANES:
                v = jnp.concatenate([v, jnp.zeros((8, LANES - width), jnp.float32)], axis=1)
            packed[pl.ds((group * 8 + HALO) * pitch + c, 8, stride=pitch), :] = v
        return carry

    lax.fori_loop(0, plan.rows // 8, fill, 0)
    main = (own + HALO) * pitch
    mine = pl.multiple_of(me * own * pitch, 8)
    local = pltpu.make_async_copy(
        packed.at[pl.ds(mine, main)], out_ref.at[me, pl.ds(0, main)], own_sem
    )
    local.start()
    copies = []
    for k in range(1, blocks):
        to = lax.rem(me + k, blocks)
        copy = pltpu.make_async_remote_copy(
            src_ref=packed.at[pl.ds(pl.multiple_of(to * own * pitch, 8), main)],
            dst_ref=out_ref.at[me, pl.ds(0, main)],
            send_sem=send.at[k],
            recv_sem=recv.at[k],
            device_id={"lon": to, "lat": band},
            device_id_type=MESH,
        )
        copy.start()
        copies.append(copy)

    def south(i):
        f, d = plan.south_to[i]
        first = (HALO + f * plan.lat + plan.lat - HALO) * pitch
        return pltpu.make_async_remote_copy(
            src_ref=packed.at[pl.ds(first, HALO * pitch)],
            dst_ref=out_ref.at[me, pl.ds(main, HALO * pitch)],
            send_sem=south_send.at[i],
            recv_sem=south_recv.at[me],
            device_id={"lon": jnp.int32(d), "lat": lax.rem(band + 1, plan.bands)},
            device_id_type=MESH,
        )

    @pl.when(band < plan.bands - 1)
    def _():
        for i in range(len(plan.south_to)):
            south(i).start()

    local.wait()
    for copy in copies:
        copy.wait()

    @pl.when(band < plan.bands - 1)
    def _():
        for i in range(len(plan.south_to)):
            south(i).wait_send()

    for d in sorted({d for _, d in plan.south_to}):

        @pl.when(jnp.logical_and(band > 0, me == d))
        def _():
            for source in range(blocks):
                pltpu.make_async_remote_copy(
                    src_ref=packed.at[pl.ds(0, HALO * pitch)],
                    dst_ref=out_ref.at[source, pl.ds(main, HALO * pitch)],
                    send_sem=south_send.at[0],
                    recv_sem=south_recv.at[source],
                    device_id={"lon": me, "lat": band - 1},
                    device_id_type=MESH,
                ).wait_recv()


def row_steps(plan, x, courant, count, marked, power, joined):
    blocks, cols, rem = plan.blocks, plan.cols, plan.rem
    lane = lax.broadcasted_iota(jnp.int32, (blocks, LANES), 1)
    tail = lane < rem
    x = x[:-1] + [jnp.where(tail, x[-1], 0.0)]

    half = 0.5 * (1.0 - courant)
    w0 = 1.0 - courant * (1.0 + half)
    w1 = courant * (1.0 + 2.0 * half)
    w2 = -courant * half
    west = pltpu.roll(x[-1], 1, 0)
    before1 = pltpu.roll(west, LANES + 1 - rem, 1) if rem > 1 else west
    before2 = pltpu.roll(west, LANES + 2 - rem, 1)
    zonal = []
    for c in range(cols):
        one, two = pltpu.roll(x[c], 1, 1), pltpu.roll(x[c], 2, 1)
        zonal.append(
            w0 * x[c]
            + w1 * jnp.where(lane < 1, before1, one)
            + w2 * jnp.where(lane < 2, before2, two)
        )
        before1, before2 = one, two

    count = jnp.where(count < 0, count + plan.lon_total, count)
    jump = count // plan.lon
    start = plan.lon - (count - jump * plan.lon)
    moved = [pltpu.roll(z, jump, 0) for z in zonal]
    western = [pltpu.roll(m, 1, 0) for m in moved]
    turned = [pltpu.roll(m, rem % LANES, 1) for m in moved]
    for c in range(cols - 1):
        joined[:, c * LANES : (c + 1) * LANES] = western[c]
    for c in range(cols + 1):
        left = western[-1] if c == 0 else turned[c - 1]
        right = turned[c] if c < cols else left
        at = (cols - 1 + c) * LANES
        joined[:, at : at + LANES] = jnp.where(tail, left, right)
    first = start // LANES
    within = start - first * LANES
    window = [
        joined[:, pl.ds(pl.multiple_of((first + c) * LANES, LANES), LANES)] for c in range(cols + 1)
    ]
    window = [pltpu.roll(w, lax.rem(LANES - within, LANES), 1) for w in window]
    keep = lane < LANES - within
    s = [jnp.where(keep, window[c], window[c + 1]) for c in range(cols)]
    s[-1] = jnp.where(tail, s[-1], 0.0)

    r128, r_rem, gain, closing, log_r = (power(7 + i) for i in range(5))
    ahead = [jnp.where(lane >= 1 << k, power(k), 0.0) for k in range(7)]
    back = [jnp.where(lane < LANES - (1 << k), power(k), 0.0) for k in range(7)]
    lane_f = lane.astype(jnp.float32)
    enter_west = jnp.exp(log_r * (lane_f + 1.0))
    enter_east = jnp.exp(log_r * (LANES - lane_f))
    enter_tail = jnp.exp(log_r * jnp.maximum(rem - lane_f, 0.0))
    p, q = [], []
    for c in range(cols):
        u, v = s[c], s[c]
        for k in range(7):
            u = u + ahead[k] * pltpu.roll(u, 1 << k, 1)
            v = v + back[k] * pltpu.roll(v, LANES - (1 << k), 1)
        p.append(u)
        q.append(v)

    def spread(column, at):
        return jnp.broadcast_to(column[:, at : at + 1], (blocks, LANES))

    ends = [spread(p[c], LANES - 1 if c < cols - 1 else rem - 1) for c in range(cols)]
    begins = [spread(q[c], 0) for c in range(cols)]

    def closed(total, sign):
        total = pltpu.roll(total, 1 if sign > 0 else blocks - 1, 0)
        for k in range(blocks.bit_length() - 1):
            by = 1 << k
            total = total + power(12 + k) * pltpu.roll(total, by if sign > 0 else blocks - by, 0)
        return total * closing

    total = ends[0]
    for c in range(1, cols):
        total = ends[c] + (r128 if c < cols - 1 else r_rem) * total
    carry = closed(total, 1)
    for c in range(cols):
        p[c] = p[c] + enter_west * carry
        carry = ends[c] + r128 * carry
    total = begins[-1]
    for c in range(cols - 2, -1, -1):
        total = begins[c] + r128 * total
    carry = closed(total, -1)
    for c in range(cols - 1, -1, -1):
        q[c] = q[c] + (enter_tail if c == cols - 1 else enter_east) * carry
        carry = begins[c] + (r_rem if c == cols - 1 else r128) * carry
    return [jnp.where(marked, gain * (p[c] + q[c] - s[c]), s[c]) for c in range(cols)]


def rows_kernel(plan, place, cx, cy, shift, mask, table, x_ref, out_ref, held, joined):
    blocks, pitch, own, cols, lat = plan.blocks, plan.pitch, plan.own, plan.cols, plan.lat
    me = place[0]
    band = place[1]

    def steps(x, t, row):
        return row_steps(
            plan, x, cx[t, row], shift[t, row], mask[0, row] == 1, lambda i: table[i, row], joined
        )

    def first_pass(slot, none):
        x = [
            x_ref[pl.ds(slot * pitch + c, blocks, stride=plan.slots * pitch), :]
            for c in range(cols)
        ]
        flat = me * own + slot - HALO
        south = slot >= own + HALO
        row = jnp.where(south, band * lat + slot - (own + 2 * HALO), band * lat + lax.rem(flat + lat, lat))
        y = steps(x, 0, jnp.maximum(row, 0))
        outside = jnp.logical_and(south, band == 0)
        for c in range(cols):
            held[slot, :, c * LANES : (c + 1) * LANES] = jnp.where(outside, 0.0, y[c])
        return none

    lax.fori_loop(0, plan.slots, first_pass, 0)

    def second_pass(m, none):
        j = lax.rem(me * own + m, lat)
        row = band * lat + j
        s0 = m + HALO
        s1 = jnp.where(j == 0, own + 3, s0 - 1)
        s2 = jnp.where(j == 0, own + 2, jnp.where(j == 1, own + 3, s0 - 2))
        c0 = jnp.where(row == 0, 0.0, cy[0, row])
        c1 = jnp.where(row == plan.lat_total - 1, 0.0, cy[0, jnp.minimum(row + 1, plan.lat_total - 1)])
        h0, h1 = 0.5 * (1.0 - c0), 0.5 * (1.0 - c1)
        a0 = 1.0 - c1 * (1.0 + h1)
        a1 = c1 * h1 + c0 * (1.0 + h0)
        a2 = -c0 * h0
        x = []
        for c in range(cols):
            at = slice(c * LANES, (c + 1) * LANES)
            x.append(a0 * held[s0, :, at] + a1 * held[s1, :, at] + a2 * held[s2, :, at])
        y = steps(x, 1, row)
        for c in range(cols):
            out_ref[pl.ds(m * pitch + c, blocks, stride=own * pitch), :] = y[c]
        return none

    lax.fori_loop(0, own, second_pass, 0)


def back_kernel(plan, coef_ref, x_ref, out_ref, got, got_south, send, recv, south_send, south_recv, own_sem):
    me = lax.axis_index("lon")
    band = lax.axis_index("lat")
    blocks, pitch, own, lat = plan.blocks, plan.pitch, plan.own, plan.lat
    size = own * pitch
    here = pl.multiple_of(me * size, 8)
    pieces = [
        (f, part) for f in range(plan.fields) for part in range(HALO // plan.unit)
    ]

    def south(i, to):
        f, part = pieces[i]
        flat = f * lat + lat - HALO + part * plan.unit
        inside = flat - (flat // own) * own
        return pltpu.make_async_remote_copy(
            src_ref=x_ref.at[to, pl.ds(inside * pitch, plan.unit * pitch)],
            dst_ref=got_south.at[pl.ds((f * HALO + part * plan.unit) * pitch, plan.unit * pitch)],
            send_sem=south_send.at[i, to],
            recv_sem=south_recv.at[i],
            device_id={"lon": jnp.int32(to), "lat": lax.rem(band + 1, plan.bands)},
            device_id_type=MESH,
        )

    def owner(i):
        f, part = pieces[i]
        return (f * lat + lat - HALO + part * plan.unit) // own

    local = pltpu.make_async_copy(x_ref.at[me], got.at[pl.ds(here, size)], own_sem)
    local.start()
    copies = []
    for k in range(1, blocks):
        to = lax.rem(me + k, blocks)
        copy = pltpu.make_async_remote_copy(
            src_ref=x_ref.at[to],
            dst_ref=got.at[pl.ds(here, size)],
            send_sem=send.at[k],
            recv_sem=recv.at[k],
            device_id={"lon": to, "lat": band},
            device_id_type=MESH,
        )
        copy.start()
        copies.append(copy)
    for i in range(len(pieces)):

        @pl.when(jnp.logical_and(band < plan.bands - 1, me == owner(i)))
        def _():
            for to in range(blocks):
                south(i, to).start()

    local.wait()
    for copy in copies:
        copy.wait()
    for i in range(len(pieces)):

        @pl.when(jnp.logical_and(band < plan.bands - 1, me == owner(i)))
        def _():
            for to in range(blocks):
                south(i, to).wait_send()

    @pl.when(band > 0)
    def _():
        for i in range(len(pieces)):
            south(i, 0).wait_recv()

    @pl.when(band == 0)
    def _():
        got_south[...] = jnp.zeros_like(got_south)

    sub = lax.broadcasted_iota(jnp.int32, (8, LANES), 0)

    def one_field(f, none):
        for g in range(lat // 8):
            a0, a1, a2 = (coef_ref[i, g * 8 : g * 8 + 8, :] for i in range(3))
            for c in range(plan.cols):
                base = (f * lat + g * 8) * pitch + c
                x0 = got[pl.ds(base, 8, stride=pitch), :]
                if g:
                    x1 = got[pl.ds(base - pitch, 8, stride=pitch), :]
                    x2 = got[pl.ds(base - 2 * pitch, 8, stride=pitch), :]
                else:
                    south2 = got_south[pl.ds(f * HALO * pitch + c, 1), :]
                    south1 = got_south[pl.ds((f * HALO + 1) * pitch + c, 1), :]
                    x1 = jnp.where(sub == 0, south1, pltpu.roll(x0, 1, 0))
                    x2 = jnp.where(
                        sub == 0, south2, jnp.where(sub == 1, south1, pltpu.roll(x0, 2, 0))
                    )
                v = a0 * x0 + a1 * x1 + a2 * x2
                width = LANES if c < plan.cols - 1 else plan.rem
                out_ref[f, 0, g * 8 : g * 8 + 8, c * LANES : c * LANES + width] = v[:, :width]
        return none

    lax.fori_loop(0, plan.fields, one_field, 0)


def body(plan, fields, frac_x, frac_y, shift_cells, polar_mask):
    blocks, pitch, own, lat = plan.blocks, plan.pitch, plan.own, plan.lat
    me = lax.axis_index("lon")
    band = lax.axis_index("lat")
    vmem = pl.BlockSpec(memory_space=pltpu.VMEM)
    smem = pl.BlockSpec(memory_space=pltpu.SMEM)
    anywhere = pl.BlockSpec(memory_space=pl.ANY)
    dma = pltpu.SemaphoreType.DMA
    spread = pl.pallas_call(
        functools.partial(spread_kernel, plan),
        out_shape=jax.ShapeDtypeStruct((blocks, plan.slots * pitch, LANES), jnp.float32),
        in_specs=[vmem],
        out_specs=anywhere,
        scratch_shapes=[
            pltpu.VMEM(((HALO + plan.rows) * pitch, LANES), jnp.float32),
            dma((blocks,)),
            dma((blocks,)),
            dma((len(plan.south_to),)),
            dma((blocks,)),
            dma,
        ],
        compiler_params=pltpu.CompilerParams(has_side_effects=True, vmem_limit_bytes=VMEM_LIMIT),
        name="to_rows",
    )(fields.reshape(plan.rows, plan.lon))

    place = jnp.stack([me, band]).astype(jnp.int32)
    filtered = pl.pallas_call(
        functools.partial(rows_kernel, plan),
        out_shape=jax.ShapeDtypeStruct((blocks * own * pitch, LANES), jnp.float32),
        in_specs=[smem] * 6 + [vmem],
        out_specs=vmem,
        scratch_shapes=[
            pltpu.VMEM((plan.slots, blocks, plan.cols * LANES), jnp.float32),
            pltpu.VMEM((blocks, 2 * plan.cols * LANES), jnp.float32),
        ],
        compiler_params=pltpu.CompilerParams(vmem_limit_bytes=VMEM_LIMIT),
        name="row_steps",
    )(
        place,
        frac_x[:, 0, :],
        frac_y[:, 0, :],
        shift_cells[:, 0, :],
        polar_mask[None],
        jnp.asarray(decay_table(plan)),
        spread.reshape(blocks * plan.slots * pitch, LANES),
    )

    faces = frac_y[SUBS - 1, 0]
    ids = jnp.arange(plan.lat_total, dtype=jnp.int32)
    c0 = jnp.where(ids == 0, 0.0, faces)
    c1 = jnp.where(ids == plan.lat_total - 1, 0.0, jnp.roll(faces, -1))
    h0, h1 = 0.5 * (1.0 - c0), 0.5 * (1.0 - c1)
    coef = jnp.stack([1.0 - c1 * (1.0 + h1), c1 * h1 + c0 * (1.0 + h0), -c0 * h0])
    coef = lax.dynamic_slice_in_dim(coef, band * lat, lat, 1)
    coef = jnp.broadcast_to(coef[:, :, None], (3, lat, LANES))

    n_pieces = plan.fields * (HALO // plan.unit)
    return pl.pallas_call(
        functools.partial(back_kernel, plan),
        out_shape=jax.ShapeDtypeStruct(fields.shape, jnp.float32),
        in_specs=[vmem, anywhere],
        out_specs=vmem,
        scratch_shapes=[
            pltpu.VMEM((plan.rows * pitch, LANES), jnp.float32),
            pltpu.VMEM((plan.fields * HALO * pitch, LANES), jnp.float32),
            dma((blocks,)),
            dma((blocks,)),
            dma((n_pieces, blocks)),
            dma((n_pieces,)),
            dma,
        ],
        compiler_params=pltpu.CompilerParams(has_side_effects=True, vmem_limit_bytes=VMEM_LIMIT),
        name="to_longitudes",
    )(coef, filtered.reshape(blocks, own * pitch, LANES))


def solution(mesh):
    def whole(fields, frac_x, frac_y, shift_cells, polar_mask):
        return jax.shard_map(
            functools.partial(body, Plan(mesh, fields.shape)),
            mesh=mesh,
            in_specs=(P(None, None, "lat", "lon"), P(), P(), P(), P()),
            out_specs=P(None, None, "lat", "lon"),
            check_vma=False,
        )(fields, frac_x, frac_y, shift_cells, polar_mask)

    return whole
```

time: 381 us -> 86.7 us (0.23)
  the two profiles are of different devices: /device:TPU:0 before, /device:TPU:9 now
where the time goes in v1:
time: 86.7 us; the launch traced here: 86.3 us
  Pallas kernels  80.5 us (93%)
  local copies, waits for them, and re-layouts  4.26 us (5%)
  other arithmetic  1.47 us (2%)
    pallas_call x1, Pallas kernels, body(): pl.pallas_call(functools.partial(rows_kernel, plan), out_shape=jax.ShapeD...  40.1 us
    pallas_call x1, Pallas kernels, body(): pl.pallas_call(functools.partial(spread_kernel, plan), out_shape=jax.Shap...  21.7 us
    pallas_call x1, Pallas kernels, body(): pl.pallas_call(functools.partial(back_kernel, plan), out_shape=jax.ShapeD...  18.6 us
    unnamed x13, local copies, waits for them, and re-layouts  2.18 us

profile of v1, /device:TPU:9, one launch (start us, length us, event | category | flops | bytes accessed | tf_op | source)
XLA Modules:
  0.0 86.3 jit_solution(8527518800910675799)
XLA Ops:
  0.0 0.0 copy-start.1
  0.0 0.0 copy-start.2
  0.0 0.0 copy-start.5
  0.0 0.0 copy-start.4
  0.0 0.0 copy-start.3
  0.0 1.2 %slice.16 = f32[1,1,1]{2,1,0:T(1,128)} slice(f32[2,1,128]{2,1,0:T(1,128)} %param.8), slice={[1:2], [0:1], [0:1]} | slice | bytes 8 | tf_op jit(solution)/shard_map/jit(_roll_static)/slice | solution.py:422
  1.2 0.1 pad_add_fusion.place
  1.3 0.7 slice_bitcast_fusion
  2.0 0.7 multiply_subtract_fusion
  2.8 0.7 multiply_add_fusion
  3.4 0.1 constant_dynamic-slice_fusion
  3.5 0.1 broadcast_in_dim.15.coef_ref
  3.6 0.0 copy-start
  3.6 1.2 %copy-done = f32[5,1,32,1440]{3,2,1,0:T(8,128)S(1)} copy-done((f32[5,1,32,1440]{3,2,1,0:T(8,128)S(1)}, f32[5,1,32,1440]{3,2,1,0:T(8,128)}, u32[]{:S(2)}) %copy-start) | copy-done | bytes 921624
  4.8 21.7 %to_rows.1 = f32[8,288,128]{2,1,0:T(8,128)S(1)} custom-call(f32[160,1440]{1,0:T(8,128)S(1)} %bitcast.20), custom_call_target="tpu_custom_call" | custom-call | tf_op jit(solution)/shard_map/to_rows/pallas_call | solution.py:380
  26.5 0.0 copy-done.1
  26.5 0.0 copy-done.2
  26.6 0.0 copy-done.5
  26.6 0.0 copy-done.4
  26.6 0.0 copy-done.3
  26.6 40.1 %row_steps.1 = f32[1920,128]{1,0:T(8,128)S(1)} custom-call(s32[2]{0:T(128)S(1)} %pad_add_fusion.place, f32[2,128]{1,0:T(2,128)S(1)} %bitcast.22, f32[2,128]{1,0:T(2,128)S(1)} %bitcast.21, s32[2,128]{1,0:T(2,128)S(1)} %bitcast.23, s32[1,128]{1,0:T(1,128)S(1)} %bitcast.24, f32[15,128]{1,0:T(8,128)S(1)} %copy-done.1, f32[2304,128]{1,0:T(8,128)S(1)} %bitcast.18), custom_call_target="tpu_custom_call" | custom-call | tf_op jit(solution)/shard_map/row_steps/pallas_call | solution.py:398
  66.7 18.6 %to_longitudes.1 = f32[5,1,32,1440]{3,2,1,0:T(8,128)S(1)} custom-call(f32[3,32,128]{2,1,0:T(8,128)S(1)} %broadcast_in_dim.15.coef_ref, f32[8,240,128]{2,1,0:T(8,128)S(1)} %bitcast.19), custom_call_target="tpu_custom_call" | custom-call | tf_op jit(solution)/shard_map/to_longitudes/pallas_call | solution.py:429
  85.4 0.9 %copy.8 = f32[5,1,32,1440]{3,2,1,0:T(8,128)} copy(f32[5,1,32,1440]{3,2,1,0:T(8,128)S(1)} %to_longitudes.1) | data formatting | bytes 1843200
  (1 shorter events, 0.0 us)
Async XLA Ops:
  0.0 26.5 %copy-start.1 = (f32[15,128]{1,0:T(8,128)S(1)}, f32[15,128]{1,0:T(8,128)}, u32[]{:S(2)}) copy-start(f32[15,128]{1,0:T(8,128)} %constant.26.clone.table) | copy-start | bytes 23044
  0.0 26.5 %copy-start.2 = (f32[2,1,128]{2,1,0:T(1,128)S(1)}, f32[2,1,128]{2,1,0:T(1,128)}, u32[]{:S(2)}) copy-start(f32[2,1,128]{2,1,0:T(1,128)} %param.8) | copy-start | bytes 3076
  0.0 26.5 %copy-start.5 = (s32[128]{0:T(128)S(1)}, s32[128]{0:T(128)}, u32[]{:S(2)}) copy-start(s32[128]{0:T(128)} %param.10) | copy-start | bytes 1540
  0.0 26.6 %copy-start.4 = (s32[2,1,128]{2,1,0:T(1,128)S(1)}, s32[2,1,128]{2,1,0:T(1,128)}, u32[]{:S(2)}) copy-start(s32[2,1,128]{2,1,0:T(1,128)} %param.9) | copy-start | bytes 3076
  0.0 26.6 %copy-start.3 = (f32[2,1,128]{2,1,0:T(1,128)S(1)}, f32[2,1,128]{2,1,0:T(1,128)}, u32[]{:S(2)}) copy-start(f32[2,1,128]{2,1,0:T(1,128)} %param.7) | copy-start | bytes 3076
  3.6 1.2 %copy-start = (f32[5,1,32,1440]{3,2,1,0:T(8,128)S(1)}, f32[5,1,32,1440]{3,2,1,0:T(8,128)}, u32[]{:S(2)}) copy-start(f32[5,1,32,1440]{3,2,1,0:T(8,128)} %param.6) | copy-start | bytes 2764804

commit v2 on v1

--- a/solution.py
+++ b/solution.py
@@ -133,7 +133,19 @@
                 ).wait_recv()
 
 
-def row_steps(plan, x, courant, count, marked, power, joined):
+def build_weights(table, row, weights, slot):
+    i = lax.broadcasted_iota(jnp.int32, (LANES, LANES), 0)
+    j = lax.broadcasted_iota(jnp.int32, (LANES, LANES), 1)
+    apart = jnp.abs(i - j).astype(jnp.float32)
+    full = table[9, row] * jnp.exp(table[11, row] * apart)
+    high = full.astype(jnp.bfloat16)
+    low = (full - high.astype(jnp.float32)).astype(jnp.bfloat16)
+    for k in range(2):
+        weights[slot, k * LANES : (k + 1) * LANES, :LANES] = high
+        weights[slot, k * LANES : (k + 1) * LANES, LANES:] = low
+
+
+def row_steps(plan, x, courant, count, marked, power, joined, weights):
     blocks, cols, rem = plan.blocks, plan.cols, plan.rem
     lane = lax.broadcasted_iota(jnp.int32, (blocks, LANES), 1)
     tail = lane < rem
@@ -179,27 +191,26 @@
     s = [jnp.where(keep, window[c], window[c + 1]) for c in range(cols)]
     s[-1] = jnp.where(tail, s[-1], 0.0)
 
-    r128, r_rem, gain, closing, log_r = (power(7 + i) for i in range(5))
-    ahead = [jnp.where(lane >= 1 << k, power(k), 0.0) for k in range(7)]
-    back = [jnp.where(lane < LANES - (1 << k), power(k), 0.0) for k in range(7)]
+    r128, r_rem = power(7), power(8)
+    closing, log_r = power(10), power(11)
     lane_f = lane.astype(jnp.float32)
     enter_west = jnp.exp(log_r * (lane_f + 1.0))
     enter_east = jnp.exp(log_r * (LANES - lane_f))
     enter_tail = jnp.exp(log_r * jnp.maximum(rem - lane_f, 0.0))
-    p, q = [], []
-    for c in range(cols):
-        u, v = s[c], s[c]
-        for k in range(7):
-            u = u + ahead[k] * pltpu.roll(u, 1 << k, 1)
-            v = v + back[k] * pltpu.roll(v, LANES - (1 << k), 1)
-        p.append(u)
-        q.append(v)
+    stacked = jnp.concatenate(s, axis=0)
+    high = stacked.astype(jnp.bfloat16)
+    low = (stacked - high.astype(jnp.float32)).astype(jnp.bfloat16)
+    product = jnp.dot(
+        jnp.concatenate([high, low], axis=1), weights, preferred_element_type=jnp.float32
+    )
+    product = product[:, :LANES] + product[:, LANES:]
+    y = [product[c * blocks : (c + 1) * blocks] for c in range(cols)]
 
     def spread(column, at):
         return jnp.broadcast_to(column[:, at : at + 1], (blocks, LANES))
 
-    ends = [spread(p[c], LANES - 1 if c < cols - 1 else rem - 1) for c in range(cols)]
-    begins = [spread(q[c], 0) for c in range(cols)]
+    ends = [spread(y[c], LANES - 1 if c < cols - 1 else rem - 1) for c in range(cols)]
+    begins = [spread(y[c], 0) for c in range(cols)]
 
     def closed(total, sign):
         total = pltpu.roll(total, 1 if sign > 0 else blocks - 1, 0)
@@ -213,69 +224,96 @@
         total = ends[c] + (r128 if c < cols - 1 else r_rem) * total
     carry = closed(total, 1)
     for c in range(cols):
-        p[c] = p[c] + enter_west * carry
+        y[c] = y[c] + enter_west * carry
         carry = ends[c] + r128 * carry
     total = begins[-1]
     for c in range(cols - 2, -1, -1):
         total = begins[c] + r128 * total
     carry = closed(total, -1)
     for c in range(cols - 1, -1, -1):
-        q[c] = q[c] + (enter_tail if c == cols - 1 else enter_east) * carry
+        y[c] = y[c] + (enter_tail if c == cols - 1 else enter_east) * carry
         carry = begins[c] + (r_rem if c == cols - 1 else r128) * carry
-    return [jnp.where(marked, gain * (p[c] + q[c] - s[c]), s[c]) for c in range(cols)]
-
-
-def rows_kernel(plan, place, cx, cy, shift, mask, table, x_ref, out_ref, held, joined):
+    return [jnp.where(marked, y[c], s[c]) for c in range(cols)]
+
+
+def face_weights(plan, cy, t, row):
+    last = plan.lat_total - 1
+    c0 = jnp.where(row == 0, 0.0, cy[t, 0, row])
+    c1 = jnp.where(row == last, 0.0, cy[t, 0, jnp.minimum(row + 1, last)])
+    h0, h1 = 0.5 * (1.0 - c0), 0.5 * (1.0 - c1)
+    return 1.0 - c1 * (1.0 + h1), c1 * h1 + c0 * (1.0 + h0), -c0 * h0
+
+
+def rows_kernel(plan, cx, cy, shift, mask, table, x_ref, out_ref, held, weights, *joined):
     blocks, pitch, own, cols, lat = plan.blocks, plan.pitch, plan.own, plan.cols, plan.lat
-    me = place[0]
-    band = place[1]
-
-    def steps(x, t, row):
+    me = lax.axis_index("lon")
+    band = lax.axis_index("lat")
+
+    def steps(x, t, row, slot, part):
         return row_steps(
-            plan, x, cx[t, row], shift[t, row], mask[0, row] == 1, lambda i: table[i, row], joined
-        )
-
-    def first_pass(slot, none):
+            plan,
+            x,
+            cx[t, 0, row],
+            shift[t, 0, row],
+            mask[row] == 1,
+            lambda i: table[i, row],
+            joined[part],
+            weights[slot],
+        )
+
+    def place(slot):
+        flat = me * own + slot - HALO
+        south = slot >= own + HALO
+        row = jnp.where(south, slot - (own + 2 * HALO), lax.rem(flat + lat, lat))
+        return south, jnp.maximum(band * lat + row, 0)
+
+    def build(slot, none):
+        build_weights(table, place(slot)[1], weights, slot)
+        return none
+
+    lax.fori_loop(0, plan.slots, build, 0)
+
+    def first_pass(slot, part):
+        south, row = place(slot)
         x = [
             x_ref[pl.ds(slot * pitch + c, blocks, stride=plan.slots * pitch), :]
             for c in range(cols)
         ]
-        flat = me * own + slot - HALO
-        south = slot >= own + HALO
-        row = jnp.where(south, band * lat + slot - (own + 2 * HALO), band * lat + lax.rem(flat + lat, lat))
-        y = steps(x, 0, jnp.maximum(row, 0))
+        y = steps(x, 0, row, slot, part)
         outside = jnp.logical_and(south, band == 0)
         for c in range(cols):
             held[slot, :, c * LANES : (c + 1) * LANES] = jnp.where(outside, 0.0, y[c])
-        return none
-
-    lax.fori_loop(0, plan.slots, first_pass, 0)
-
-    def second_pass(m, none):
+
+    def second_pass(m, part):
         j = lax.rem(me * own + m, lat)
         row = band * lat + j
         s0 = m + HALO
         s1 = jnp.where(j == 0, own + 3, s0 - 1)
         s2 = jnp.where(j == 0, own + 2, jnp.where(j == 1, own + 3, s0 - 2))
-        c0 = jnp.where(row == 0, 0.0, cy[0, row])
-        c1 = jnp.where(row == plan.lat_total - 1, 0.0, cy[0, jnp.minimum(row + 1, plan.lat_total - 1)])
-        h0, h1 = 0.5 * (1.0 - c0), 0.5 * (1.0 - c1)
-        a0 = 1.0 - c1 * (1.0 + h1)
-        a1 = c1 * h1 + c0 * (1.0 + h0)
-        a2 = -c0 * h0
+        a0, a1, a2 = face_weights(plan, cy, 0, row)
         x = []
         for c in range(cols):
             at = slice(c * LANES, (c + 1) * LANES)
             x.append(a0 * held[s0, :, at] + a1 * held[s1, :, at] + a2 * held[s2, :, at])
-        y = steps(x, 1, row)
+        y = steps(x, 1, row, s0, part)
         for c in range(cols):
             out_ref[pl.ds(m * pitch + c, blocks, stride=own * pitch), :] = y[c]
-        return none
-
-    lax.fori_loop(0, own, second_pass, 0)
-
-
-def back_kernel(plan, coef_ref, x_ref, out_ref, got, got_south, send, recv, south_send, south_recv, own_sem):
+
+    def loop(count, each):
+        width = 2 if count % 2 == 0 else 1
+
+        def step(i, none):
+            for part in range(width):
+                each(i * width + part, part)
+            return none
+
+        lax.fori_loop(0, count // width, step, 0)
+
+    loop(plan.slots, first_pass)
+    loop(own, second_pass)
+
+
+def back_kernel(plan, cy, x_ref, out_ref, coef_ref, got, got_south, send, recv, south_send, south_recv, own_sem):
     me = lax.axis_index("lon")
     band = lax.axis_index("lat")
     blocks, pitch, own, lat = plan.blocks, plan.pitch, plan.own, plan.lat
@@ -323,6 +361,10 @@
         def _():
             for to in range(blocks):
                 south(i, to).start()
+
+    for j in range(lat):
+        for i, weight in enumerate(face_weights(plan, cy, SUBS - 1, band * lat + j)):
+            coef_ref[i, j : j + 1, :] = jnp.full((1, LANES), weight, jnp.float32)
 
     local.wait()
     for copy in copies:
@@ -371,8 +413,6 @@
 
 def body(plan, fields, frac_x, frac_y, shift_cells, polar_mask):
     blocks, pitch, own, lat = plan.blocks, plan.pitch, plan.own, plan.lat
-    me = lax.axis_index("lon")
-    band = lax.axis_index("lat")
     vmem = pl.BlockSpec(memory_space=pltpu.VMEM)
     smem = pl.BlockSpec(memory_space=pltpu.SMEM)
     anywhere = pl.BlockSpec(memory_space=pl.ANY)
@@ -394,44 +434,36 @@
         name="to_rows",
     )(fields.reshape(plan.rows, plan.lon))
 
-    place = jnp.stack([me, band]).astype(jnp.int32)
     filtered = pl.pallas_call(
         functools.partial(rows_kernel, plan),
         out_shape=jax.ShapeDtypeStruct((blocks * own * pitch, LANES), jnp.float32),
-        in_specs=[smem] * 6 + [vmem],
+        in_specs=[smem] * 5 + [vmem],
         out_specs=vmem,
         scratch_shapes=[
             pltpu.VMEM((plan.slots, blocks, plan.cols * LANES), jnp.float32),
+            pltpu.VMEM((plan.slots, 2 * LANES, 2 * LANES), jnp.bfloat16),
+            pltpu.VMEM((blocks, 2 * plan.cols * LANES), jnp.float32),
             pltpu.VMEM((blocks, 2 * plan.cols * LANES), jnp.float32),
         ],
         compiler_params=pltpu.CompilerParams(vmem_limit_bytes=VMEM_LIMIT),
         name="row_steps",
     )(
-        place,
-        frac_x[:, 0, :],
-        frac_y[:, 0, :],
-        shift_cells[:, 0, :],
-        polar_mask[None],
+        frac_x,
+        frac_y,
+        shift_cells,
+        polar_mask,
         jnp.asarray(decay_table(plan)),
         spread.reshape(blocks * plan.slots * pitch, LANES),
     )
-
-    faces = frac_y[SUBS - 1, 0]
-    ids = jnp.arange(plan.lat_total, dtype=jnp.int32)
-    c0 = jnp.where(ids == 0, 0.0, faces)
-    c1 = jnp.where(ids == plan.lat_total - 1, 0.0, jnp.roll(faces, -1))
-    h0, h1 = 0.5 * (1.0 - c0), 0.5 * (1.0 - c1)
-    coef = jnp.stack([1.0 - c1 * (1.0 + h1), c1 * h1 + c0 * (1.0 + h0), -c0 * h0])
-    coef = lax.dynamic_slice_in_dim(coef, band * lat, lat, 1)
-    coef = jnp.broadcast_to(coef[:, :, None], (3, lat, LANES))
 
     n_pieces = plan.fields * (HALO // plan.unit)
     return pl.pallas_call(
         functools.partial(back_kernel, plan),
         out_shape=jax.ShapeDtypeStruct(fields.shape, jnp.float32),
-        in_specs=[vmem, anywhere],
+        in_specs=[smem, anywhere],
         out_specs=vmem,
         scratch_shapes=[
+            pltpu.VMEM((3, lat, LANES), jnp.float32),
             pltpu.VMEM((plan.rows * pitch, LANES), jnp.float32),
             pltpu.VMEM((plan.fields * HALO * pitch, LANES), jnp.float32),
             dma((blocks,)),
@@ -442,7 +474,7 @@
         ],
         compiler_params=pltpu.CompilerParams(has_side_effects=True, vmem_limit_bytes=VMEM_LIMIT),
         name="to_longitudes",
-    )(coef, filtered.reshape(blocks, own * pitch, LANES))
+    )(frac_y, filtered.reshape(blocks, own * pitch, LANES))
 
 
 def solution(mesh):

time: 86.7 us -> 58.8 us (0.68)
  Pallas kernels: 80.5 us -> 56.2 us
  local copies, waits for them, and re-layouts: 4.26 us -> 2.19 us
  other arithmetic: 1.47 us -> 0 us
    pallas_call x1, Pallas kernels: 40.1 us -> 15.2 us  [body(): pl.pallas_call(functools.partial(rows_kernel, plan), out_shape=jax.ShapeD...]
    slice x1 -> x0, local copies, waits for them, and re-layouts: 1.21 us -> none  [body(): c1 = jnp.where(ids == plan.lat_total - 1, 0.0, jnp.roll(faces, -1))]
where the time goes in v2:
time: 58.8 us; the launch traced here: 58.5 us
  Pallas kernels  56.2 us (96%)
  local copies, waits for them, and re-layouts  2.19 us (4%)
    pallas_call x1, Pallas kernels, body(): pl.pallas_call(functools.partial(spread_kernel, plan), out_shape=jax.Shap...  21.7 us
    pallas_call x1, Pallas kernels, body(): pl.pallas_call(functools.partial(back_kernel, plan), out_shape=jax.ShapeD...  19.3 us
    pallas_call x1, Pallas kernels, body(): pl.pallas_call(functools.partial(rows_kernel, plan), out_shape=jax.ShapeD...  15.2 us
    unnamed x13, local copies, waits for them, and re-layouts  2.19 us

profile of v2, /device:TPU:9, one launch (start us, length us, event | category | flops | bytes accessed | tf_op | source)
XLA Modules:
  0.0 58.5 jit_solution(14730878422352486656)
XLA Ops:
  0.0 0.0 copy-start.2
  0.0 0.0 copy-start.5
  0.0 0.0 copy-start
  0.0 1.2 %copy-done = f32[5,1,32,1440]{3,2,1,0:T(8,128)S(1)} copy-done((f32[5,1,32,1440]{3,2,1,0:T(8,128)S(1)}, f32[5,1,32,1440]{3,2,1,0:T(8,128)}, u32[]{:S(2)}) %copy-start) | copy-done | bytes 921624
  1.2 0.0 copy-start.1
  1.2 0.0 copy-start.3
  1.2 0.0 copy-start.4
  1.2 21.7 %to_rows.1 = f32[8,288,128]{2,1,0:T(8,128)S(1)} custom-call(f32[160,1440]{1,0:T(8,128)S(1)} %bitcast.5), custom_call_target="tpu_custom_call" | custom-call | tf_op jit(solution)/shard_map/to_rows/pallas_call | solution.py:420
  23.0 0.0 copy-done.2
  23.0 0.0 copy-done.5
  23.0 0.0 copy-done.1
  23.0 0.0 copy-done.3
  23.0 0.0 copy-done.4
  23.0 15.2 %row_steps.1 = f32[1920,128]{1,0:T(8,128)S(1)} custom-call(f32[2,1,128]{2,1,0:T(1,128)S(1)} %copy-done.3, f32[2,1,128]{2,1,0:T(1,128)S(1)} %copy-done.2, s32[2,1,128]{2,1,0:T(1,128)S(1)} %copy-done.4, s32[128]{0:T(128)S(1)} %copy-done.5, f32[15,128]{1,0:T(8,128)S(1)} %copy-done.1, f32[2304,128]{1,0:T(8,128)S(1)} %bitcast.3), custom_call_target="tpu_custom_call" | custom-call | tf_op jit(solution)/shard_map/row_steps/pallas_call | solution.py:437
  38.3 19.3 %to_longitudes.1 = f32[5,1,32,1440]{3,2,1,0:T(8,128)S(1)} custom-call(f32[2,1,128]{2,1,0:T(1,128)S(1)} %copy-done.2, f32[8,240,128]{2,1,0:T(8,128)S(1)} %bitcast.4), custom_call_target="tpu_custom_call" | custom-call | tf_op jit(solution)/shard_map/to_longitudes/pallas_call | solution.py:460
  57.5 0.9 %copy.8 = f32[5,1,32,1440]{3,2,1,0:T(8,128)} copy(f32[5,1,32,1440]{3,2,1,0:T(8,128)S(1)} %to_longitudes.1) | data formatting | bytes 1843200
Async XLA Ops:
  0.0 23.0 %copy-start.2 = (f32[2,1,128]{2,1,0:T(1,128)S(1)}, f32[2,1,128]{2,1,0:T(1,128)}, u32[]{:S(2)}) copy-start(f32[2,1,128]{2,1,0:T(1,128)} %cy.3) | copy-start | bytes 3076
  0.0 23.0 %copy-start.5 = (s32[128]{0:T(128)S(1)}, s32[128]{0:T(128)}, u32[]{:S(2)}) copy-start(s32[128]{0:T(128)} %mask.1) | copy-start | bytes 1540
  0.0 1.2 %copy-start = (f32[5,1,32,1440]{3,2,1,0:T(8,128)S(1)}, f32[5,1,32,1440]{3,2,1,0:T(8,128)}, u32[]{:S(2)}) copy-start(f32[5,1,32,1440]{3,2,1,0:T(8,128)} %param.6) | copy-start | bytes 2764804
  1.2 21.8 %copy-start.1 = (f32[15,128]{1,0:T(8,128)S(1)}, f32[15,128]{1,0:T(8,128)}, u32[]{:S(2)}) copy-start(f32[15,128]{1,0:T(8,128)} %constant.2.clone.table) | copy-start | bytes 23044
  1.2 21.8 %copy-start.3 = (f32[2,1,128]{2,1,0:T(1,128)S(1)}, f32[2,1,128]{2,1,0:T(1,128)}, u32[]{:S(2)}) copy-start(f32[2,1,128]{2,1,0:T(1,128)} %cx.1) | copy-start | bytes 3076
  1.2 21.8 %copy-start.4 = (s32[2,1,128]{2,1,0:T(1,128)S(1)}, s32[2,1,128]{2,1,0:T(1,128)}, u32[]{:S(2)}) copy-start(s32[2,1,128]{2,1,0:T(1,128)} %shift.1) | copy-start | bytes 3076

commit v3 on v2

v3 whole, which is shorter than its diff:
```python
import functools
import math

import jax
import jax.numpy as jnp
import numpy as np
from jax import lax
from jax.experimental import pallas as pl
from jax.experimental.pallas import tpu as pltpu
from jax.sharding import PartitionSpec as P

SUBS = 2
LANES = 128
HALO = 2
MESH = pl.DeviceIdType.MESH
VMEM_LIMIT = 48 * 1024 * 1024


class Plan:
    def __init__(self, mesh, fields_shape):
        self.blocks = mesh.shape["lon"]
        self.bands = mesh.shape["lat"]
        self.fields, _, self.lat_total, self.lon_total = fields_shape
        self.lat = self.lat_total // self.bands
        self.lon = self.lon_total // self.blocks
        self.cols = -(-self.lon // LANES)
        self.rem = self.lon - LANES * (self.cols - 1)
        self.rows = self.fields * self.lat
        self.own = self.rows // self.blocks
        pitch = self.cols
        while (self.own * pitch) % 8 or (HALO * pitch) % 8:
            pitch += 1
        self.pitch = pitch
        self.slots = self.own + 2 * HALO
        self.group = 4 if self.own % 4 == 0 else self.own
        self.groups = self.own // self.group
        self.unit = 2 if self.own % 2 == 0 else 1
        assert self.rows % self.blocks == 0 and self.own <= self.lat
        assert self.blocks & (self.blocks - 1) == 0 and self.blocks % 8 == 0 and self.lat % 8 == 0
        self.south_to = [
            (f, d)
            for f in range(self.fields)
            for d in sorted({f * self.lat // self.own, (f * self.lat + 1) // self.own})
        ]


def decay_table(plan):
    rows = np.arange(plan.lat_total, dtype=np.float64)
    phi = math.pi * (rows + 0.5) / plan.lat_total - math.pi / 2
    b = np.cos(phi) / math.sin(math.pi * (plan.lat - 0.5) / plan.lat_total)
    log_r = -2.0 * np.arcsinh(b)
    r = np.exp(log_r)
    lines = [np.exp(log_r * 2**k) for k in range(7)]
    lines += [np.exp(log_r * LANES), np.exp(log_r * plan.rem)]
    lines += [(1 - r) / (1 + r), 1 / (1 - np.exp(log_r * plan.lon_total)), log_r]
    lines += [np.exp(log_r * plan.lon * 2**k) for k in range(plan.blocks.bit_length() - 1)]
    table = np.stack(lines).astype(np.float32)
    return np.where(np.abs(table) < 1.2e-38, np.float32(0), table)


def build_weights(table, row, weights, slot):
    i = lax.broadcasted_iota(jnp.int32, (LANES, LANES), 0)
    j = lax.broadcasted_iota(jnp.int32, (LANES, LANES), 1)
    apart = jnp.abs(i - j).astype(jnp.float32)
    full = table[9, row] * jnp.exp(table[11, row] * apart)
    high = full.astype(jnp.bfloat16)
    low = (full - high.astype(jnp.float32)).astype(jnp.bfloat16)
    for k in range(2):
        weights[slot, k * LANES : (k + 1) * LANES, :LANES] = high
        weights[slot, k * LANES : (k + 1) * LANES, LANES:] = low


def row_steps(plan, x, courant, count, marked, power, weights):
    blocks, cols, rem = plan.blocks, plan.cols, plan.rem
    lane = lax.broadcasted_iota(jnp.int32, (blocks, LANES), 1)
    tail = lane < rem
    x = x[:-1] + [jnp.where(tail, x[-1], 0.0)]

    half = 0.5 * (1.0 - courant)
    w0 = 1.0 - courant * (1.0 + half)
    w1 = courant * (1.0 + 2.0 * half)
    w2 = -courant * half
    west = pltpu.roll(x[-1], 1, 0)
    before1 = pltpu.roll(west, LANES + 1 - rem, 1) if rem > 1 else west
    before2 = pltpu.roll(west, LANES + 2 - rem, 1)
    zonal = []
    for c in range(cols):
        one, two = pltpu.roll(x[c], 1, 1), pltpu.roll(x[c], 2, 1)
        zonal.append(
            w0 * x[c]
            + w1 * jnp.where(lane < 1, before1, one)
            + w2 * jnp.where(lane < 2, before2, two)
        )
        before1, before2 = one, two

    count = lax.rem(count + plan.lon_total, plan.lon_total)
    moved = [pltpu.roll(z, lax.div(count, plan.lon), 0) for z in zonal]
    start = plan.lon - lax.rem(count, plan.lon)
    western = [pltpu.roll(m, 1, 0) for m in moved]
    turned = [pltpu.roll(m, rem % LANES, 1) for m in moved]
    window = western[:-1]
    for c in range(cols + 1):
        left = western[-1] if c == 0 else turned[c - 1]
        right = turned[c] if c < cols else left
        window.append(jnp.where(tail, left, right))
    first = jnp.full((blocks, LANES), start, jnp.int32) >> 7
    for k in reversed(range((cols - 1).bit_length())):
        by = 1 << k
        taken = (first & by) == by
        window = [
            jnp.where(taken, window[i + by], window[i]) if i + by < len(window) else window[i]
            for i in range(min(len(window), cols + by))
        ]
    within = start & (LANES - 1)
    window = [pltpu.roll(w, (LANES - within) & (LANES - 1), 1) for w in window]
    keep = lane < LANES - jnp.full((blocks, LANES), within, jnp.int32)
    s = [jnp.where(keep, window[c], window[c + 1]) for c in range(cols)]
    s[-1] = jnp.where(tail, s[-1], 0.0)

    r128, r_rem = power(7), power(8)
    closing, log_r = power(10), power(11)
    lane_f = lane.astype(jnp.float32)
    enter_west = jnp.exp(log_r * (lane_f + 1.0))
    enter_east = jnp.exp(log_r * (LANES - lane_f))
    enter_tail = jnp.exp(log_r * jnp.maximum(rem - lane_f, 0.0))
    stacked = jnp.concatenate(s, axis=0)
    high = stacked.astype(jnp.bfloat16)
    low = (stacked - high.astype(jnp.float32)).astype(jnp.bfloat16)
    product = jnp.dot(
        jnp.concatenate([high, low], axis=1), weights, preferred_element_type=jnp.float32
    )
    product = product[:, :LANES] + product[:, LANES:]
    y = [product[c * blocks : (c + 1) * blocks] for c in range(cols)]

    def spread(column, at):
        return jnp.broadcast_to(column[:, at : at + 1], (blocks, LANES))

    ends = [spread(y[c], LANES - 1 if c < cols - 1 else rem - 1) for c in range(cols)]
    begins = [spread(y[c], 0) for c in range(cols)]

    def closed(total, sign):
        total = pltpu.roll(total, 1 if sign > 0 else blocks - 1, 0)
        for k in range(blocks.bit_length() - 1):
            by = 1 << k
            total = total + power(12 + k) * pltpu.roll(total, by if sign > 0 else blocks - by, 0)
        return total * closing

    total = ends[0]
    for c in range(1, cols):
        total = ends[c] + (r128 if c < cols - 1 else r_rem) * total
    carry = closed(total, 1)
    for c in range(cols):
        y[c] = y[c] + enter_west * carry
        carry = ends[c] + r128 * carry
    total = begins[-1]
    for c in range(cols - 2, -1, -1):
        total = begins[c] + r128 * total
    carry = closed(total, -1)
    for c in range(cols - 1, -1, -1):
        y[c] = y[c] + (enter_tail if c == cols - 1 else enter_east) * carry
        carry = begins[c] + (r_rem if c == cols - 1 else r128) * carry
    filtered = jnp.full((blocks, LANES), marked, jnp.int32) == 1
    return [jnp.where(filtered, y[c], s[c]) for c in range(cols)]


def face_weights(plan, cy, t, row):
    last = plan.lat_total - 1
    c0 = jnp.where(row == 0, 0.0, cy[t, 0, row])
    c1 = jnp.where(row == last, 0.0, cy[t, 0, jnp.minimum(row + 1, last)])
    h0, h1 = 0.5 * (1.0 - c0), 0.5 * (1.0 - c1)
    return 1.0 - c1 * (1.0 + h1), c1 * h1 + c0 * (1.0 + h0), -c0 * h0


def start_all(copies):
    for copy in copies:
        copy.start()


def kernel(
    plan, cx, cy, shift, mask, table, x_ref, out_ref,
    packed, arrived, held, weights, ready, got, got_south, coef,
    in_send, in_recv, halo_send, halo_recv, south_in_send, south_in_recv,
    out_send, out_recv, own_out, south_out_send, south_out_recv, own_in,
):
    blocks, pitch, own, cols, lat = plan.blocks, plan.pitch, plan.own, plan.cols, plan.lat
    group, groups, slots = plan.group, plan.groups, plan.slots
    me = lax.axis_index("lon")
    band = lax.axis_index("lat")
    has_north = band < plan.bands - 1
    north = lax.rem(band + 1, plan.bands)

    def lines(first, count):
        return pl.ds(pl.multiple_of(first * pitch, 8), count * pitch)

    packed[0 : HALO * pitch, :] = jnp.zeros((HALO * pitch, LANES), jnp.float32)

    def fill(part, none):
        for c in range(cols):
            width = LANES if c < cols - 1 else plan.rem
            v = x_ref[pl.ds(pl.multiple_of(part * 8, 8), 8), c * LANES : c * LANES + width]
            if width < LANES:
                v = jnp.concatenate([v, jnp.zeros((8, LANES - width), jnp.float32)], axis=1)
            packed[pl.ds((part * 8 + HALO) * pitch + c, 8, stride=pitch), :] = v
        return none

    lax.fori_loop(0, plan.rows // 8, fill, 0)

    def peer(k):
        return lax.rem(me + k, blocks)

    def halo_in(k):
        return pltpu.make_async_remote_copy(
            src_ref=packed.at[lines(peer(k) * own, HALO)],
            dst_ref=arrived.at[lines(me * slots, HALO)],
            send_sem=halo_send.at[k],
            recv_sem=halo_recv.at[k],
            device_id={"lon": peer(k), "lat": band},
            device_id_type=MESH,
        )

    def group_in(k, g):
        return pltpu.make_async_remote_copy(
            src_ref=packed.at[lines(peer(k) * own + HALO + g * group, group)],
            dst_ref=arrived.at[lines(me * slots + HALO + g * group, group)],
            send_sem=in_send.at[k, g],
            recv_sem=in_recv.at[k, g],
            device_id={"lon": peer(k), "lat": band},
            device_id_type=MESH,
        )

    def south_in(i):
        f, d = plan.south_to[i]
        return pltpu.make_async_remote_copy(
            src_ref=packed.at[lines(HALO + f * lat + lat - HALO, HALO)],
            dst_ref=arrived.at[lines(me * slots + own + HALO, HALO)],
            send_sem=south_in_send.at[i],
            recv_sem=south_in_recv.at[me],
            device_id={"lon": jnp.int32(d), "lat": north},
            device_id_type=MESH,
        )

    local = pltpu.make_async_copy(
        packed.at[lines(me * own, own + HALO)], arrived.at[lines(me * slots, own + HALO)], own_in
    )
    local.start()
    start_all([halo_in(k) for k in range(1, blocks)])

    @pl.when(has_north)
    def _():
        start_all([south_in(i) for i in range(len(plan.south_to))])

    for g in range(groups):
        start_all([group_in(k, g) for k in range(1, blocks)])

    def place(slot):
        flat = me * own + slot - HALO
        south = slot >= own + HALO
        row = jnp.where(south, slot - (own + 2 * HALO), lax.rem(flat + lat, lat))
        return south, jnp.maximum(band * lat + row, 0)

    def build(slot, none):
        build_weights(table, place(slot)[1], weights, slot)
        return none

    lax.fori_loop(0, slots, build, 0)
    for j in range(lat):
        for i, weight in enumerate(face_weights(plan, cy, SUBS - 1, band * lat + j)):
            coef[i, j : j + 1, :] = jnp.full((1, LANES), weight, jnp.float32)

    def steps(x, t, row, slot):
        return row_steps(
            plan,
            x,
            cx[t, 0, row],
            shift[t, 0, row],
            mask[row],
            lambda i: table[i, row],
            weights[slot],
        )

    def first_pass(slot):
        south, row = place(slot)
        x = [arrived[pl.ds(slot * pitch + c, blocks, stride=slots * pitch), :] for c in range(cols)]
        y = steps(x, 0, row, slot)
        outside = jnp.logical_and(south, band == 0)
        for c in range(cols):
            held[slot, :, c * LANES : (c + 1) * LANES] = jnp.where(outside, 0.0, y[c])

    def second_pass(m):
        j = lax.rem(me * own + m, lat)
        row = band * lat + j
        s0 = m + HALO
        s1 = jnp.where(j == 0, own + 3, s0 - 1)
        s2 = jnp.where(j == 0, own + 2, jnp.where(j == 1, own + 3, s0 - 2))
        a0, a1, a2 = face_weights(plan, cy, 0, row)
        x = []
        for c in range(cols):
            at = slice(c * LANES, (c + 1) * LANES)
            x.append(a0 * held[s0, :, at] + a1 * held[s1, :, at] + a2 * held[s2, :, at])
        y = steps(x, 1, row, s0)
        for c in range(cols):
            ready[pl.ds(m * pitch + c, blocks, stride=own * pitch), :] = y[c]

    def loop(count, each):
        width = 2 if count % 2 == 0 else 1

        def step(i, none):
            for part in range(width):
                each(i * width + part)
            return none

        lax.fori_loop(0, count // width, step, 0)

    def own_back(g):
        return pltpu.make_async_copy(
            ready.at[lines(me * own + g * group, group)],
            got.at[lines(me * own + g * group, group)],
            own_out.at[g],
        )

    def group_back(k, g):
        return pltpu.make_async_remote_copy(
            src_ref=ready.at[lines(peer(k) * own + g * group, group)],
            dst_ref=got.at[lines(me * own + g * group, group)],
            send_sem=out_send.at[k, g],
            recv_sem=out_recv.at[k, g],
            device_id={"lon": peer(k), "lat": band},
            device_id_type=MESH,
        )

    pieces = [(f, part) for f in range(plan.fields) for part in range(HALO // plan.unit)]

    def piece_row(i):
        f, part = pieces[i]
        return f * lat + lat - HALO + part * plan.unit

    def south_back(i, to):
        f, part = pieces[i]
        inside = piece_row(i) % own
        return pltpu.make_async_remote_copy(
            src_ref=ready.at[lines(to * own + inside, plan.unit)],
            dst_ref=got_south.at[lines(f * HALO + part * plan.unit, plan.unit)],
            send_sem=south_out_send.at[i, to],
            recv_sem=south_out_recv.at[i],
            device_id={"lon": jnp.int32(to), "lat": north},
            device_id_type=MESH,
        )

    def sends_south(i):
        return jnp.logical_and(has_north, me == piece_row(i) // own)

    local.wait()
    for k in range(1, blocks):
        halo_in(k).wait_recv()
    for d in sorted({d for _, d in plan.south_to}):

        @pl.when(jnp.logical_and(band > 0, me == d))
        def _():
            for source in range(blocks):
                pltpu.make_async_remote_copy(
                    src_ref=packed.at[lines(0, HALO)],
                    dst_ref=arrived.at[lines(source * slots + own + HALO, HALO)],
                    send_sem=south_in_send.at[0],
                    recv_sem=south_in_recv.at[source],
                    device_id={"lon": me, "lat": lax.rem(band + plan.bands - 1, plan.bands)},
                    device_id_type=MESH,
                ).wait_recv()

    loop(2 * HALO, lambda i: first_pass(jnp.where(i < HALO, i, i + own)))

    def one_group(g, none):
        for k in range(1, blocks):
            group_in(k, g).wait_recv()
        loop(group, lambda i: first_pass(HALO + g * group + i))
        loop(group, lambda i: second_pass(g * group + i))
        own_back(g).start()
        start_all([group_back(k, g) for k in range(1, blocks)])
        for i in range(len(pieces)):

            @pl.when(jnp.logical_and(sends_south(i), g == piece_row(i) % own // group))
            def _():
                start_all([south_back(i, to) for to in range(blocks)])

        return none

    lax.fori_loop(0, groups, one_group, 0)

    for k in range(1, blocks):
        halo_in(k).wait_send()
        for g in range(groups):
            group_in(k, g).wait_send()

    @pl.when(has_north)
    def _():
        for i in range(len(plan.south_to)):
            south_in(i).wait_send()

    for g in range(groups):
        own_back(g).wait()
        for k in range(1, blocks):
            group_back(k, g).wait()
    for i in range(len(pieces)):

        @pl.when(sends_south(i))
        def _():
            for to in range(blocks):
                south_back(i, to).wait_send()

    @pl.when(band > 0)
    def _():
        for i in range(len(pieces)):
            south_back(i, 0).wait_recv()

    @pl.when(band == 0)
    def _():
        got_south[...] = jnp.zeros_like(got_south)

    sub = lax.broadcasted_iota(jnp.int32, (8, LANES), 0)

    def one_field(f, none):
        for g in range(lat // 8):
            a0, a1, a2 = (coef[i, g * 8 : g * 8 + 8, :] for i in range(3))
            for c in range(cols):
                base = (f * lat + g * 8) * pitch + c
                x0 = got[pl.ds(base, 8, stride=pitch), :]
                if g:
                    x1 = got[pl.ds(base - pitch, 8, stride=pitch), :]
                    x2 = got[pl.ds(base - 2 * pitch, 8, stride=pitch), :]
                else:
                    south2 = got_south[pl.ds(f * HALO * pitch + c, 1), :]
                    south1 = got_south[pl.ds((f * HALO + 1) * pitch + c, 1), :]
                    x1 = jnp.where(sub == 0, south1, pltpu.roll(x0, 1, 0))
                    x2 = jnp.where(
                        sub == 0, south2, jnp.where(sub == 1, south1, pltpu.roll(x0, 2, 0))
                    )
                v = a0 * x0 + a1 * x1 + a2 * x2
                width = LANES if c < cols - 1 else plan.rem
                out_ref[f, 0, g * 8 : g * 8 + 8, c * LANES : c * LANES + width] = v[:, :width]
        return none

    lax.fori_loop(0, plan.fields, one_field, 0)


def body(plan, fields, frac_x, frac_y, shift_cells, polar_mask):
    blocks, pitch, own, lat = plan.blocks, plan.pitch, plan.own, plan.lat
    vmem = pl.BlockSpec(memory_space=pltpu.VMEM)
    smem = pl.BlockSpec(memory_space=pltpu.SMEM)
    dma = pltpu.SemaphoreType.DMA
    n_pieces = plan.fields * (HALO // plan.unit)

    def lines(rows):
        return pltpu.VMEM((rows * pitch, LANES), jnp.float32)

    return pl.pallas_call(
        functools.partial(kernel, plan),
        out_shape=jax.ShapeDtypeStruct(fields.shape, jnp.float32),
        in_specs=[smem] * 5 + [vmem],
        out_specs=vmem,
        scratch_shapes=[
            lines(HALO + plan.rows),
            lines(blocks * plan.slots),
            pltpu.VMEM((plan.slots, blocks, plan.cols * LANES), jnp.float32),
            pltpu.VMEM((plan.slots, 2 * LANES, 2 * LANES), jnp.bfloat16),
            lines(blocks * own),
            lines(plan.rows),
            lines(plan.fields * HALO),
            pltpu.VMEM((3, lat, LANES), jnp.float32),
            dma((blocks, plan.groups)),
            dma((blocks, plan.groups)),
            dma((blocks,)),
            dma((blocks,)),
            dma((len(plan.south_to),)),
            dma((blocks,)),
            dma((blocks, plan.groups)),
            dma((blocks, plan.groups)),
            dma((plan.groups,)),
            dma((n_pieces, blocks)),
            dma((n_pieces,)),
            dma,
        ],
        compiler_params=pltpu.CompilerParams(has_side_effects=True, vmem_limit_bytes=VMEM_LIMIT),
        name="transport",
    )(
        frac_x,
        frac_y,
        shift_cells,
        polar_mask,
        jnp.asarray(decay_table(plan)),
        fields.reshape(plan.rows, plan.lon),
    )


def solution(mesh):
    def whole(fields, frac_x, frac_y, shift_cells, polar_mask):
        return jax.shard_map(
            functools.partial(body, Plan(mesh, fields.shape)),
            mesh=mesh,
            in_specs=(P(None, None, "lat", "lon"), P(), P(), P(), P()),
            out_specs=P(None, None, "lat", "lon"),
            check_vma=False,
        )(fields, frac_x, frac_y, shift_cells, polar_mask)

    return whole
```

time: 58.8 us -> 41.1 us (0.70)
  Pallas kernels: 56.2 us -> 35.9 us
  local copies, waits for them, and re-layouts: 2.19 us -> 4.89 us
    pallas_call x3 -> x1, Pallas kernels: 56.2 us -> 35.9 us  [body(): pl.pallas_call(functools.partial(kernel, plan), out_shape=jax.ShapeDtypeS...]
    unnamed x13, local copies, waits for them, and re-layouts: 2.19 us -> 4.89 us
where the time goes in v3:
time: 41.1 us; the launch traced here: 40.8 us
  Pallas kernels  35.9 us (87%)
  local copies, waits for them, and re-layouts  4.89 us (12%)
    pallas_call x1, Pallas kernels, body(): pl.pallas_call(functools.partial(kernel, plan), out_shape=jax.ShapeDtypeS...  35.9 us
    unnamed x13, local copies, waits for them, and re-layouts  4.89 us

profile of v3, /device:TPU:9, one launch (start us, length us, event | category | flops | bytes accessed | tf_op | source)
XLA Modules:
  0.0 40.8 jit_solution(5910357447383502609)
XLA Ops:
  0.0 0.0 copy-start.5
  0.0 0.0 copy-start.2
  0.0 0.7 %copy-done.5 = s32[128]{0:T(128)S(1)} copy-done((s32[128]{0:T(128)S(1)}, s32[128]{0:T(128)}, u32[]{:S(2)}) %copy-start.5) | copy-done | bytes 536
  0.7 0.0 copy-done.2
  0.7 0.0 copy-start
  0.7 1.2 %copy-done = f32[5,1,32,1440]{3,2,1,0:T(8,128)S(1)} copy-done((f32[5,1,32,1440]{3,2,1,0:T(8,128)S(1)}, f32[5,1,32,1440]{3,2,1,0:T(8,128)}, u32[]{:S(2)}) %copy-start) | copy-done | bytes 921624
  1.9 0.0 copy-start.1
  1.9 0.7 %copy-done.1 = f32[15,128]{1,0:T(8,128)S(1)} copy-done((f32[15,128]{1,0:T(8,128)S(1)}, f32[15,128]{1,0:T(8,128)}, u32[]{:S(2)}) %copy-start.1) | copy-done | bytes 7704
  2.6 0.0 copy-start.3
  2.6 0.7 %copy-done.3 = f32[2,1,128]{2,1,0:T(1,128)S(1)} copy-done((f32[2,1,128]{2,1,0:T(1,128)S(1)}, f32[2,1,128]{2,1,0:T(1,128)}, u32[]{:S(2)}) %copy-start.3) | copy-done | bytes 1048
  3.3 0.0 copy-start.4
  3.3 0.7 %copy-done.4 = s32[2,1,128]{2,1,0:T(1,128)S(1)} copy-done((s32[2,1,128]{2,1,0:T(1,128)S(1)}, s32[2,1,128]{2,1,0:T(1,128)}, u32[]{:S(2)}) %copy-start.4) | copy-done | bytes 1048
  4.0 35.9 %transport.1 = f32[5,1,32,1440]{3,2,1,0:T(8,128)S(1)} custom-call(f32[2,1,128]{2,1,0:T(1,128)S(1)} %copy-done.2, f32[2,1,128]{2,1,0:T(1,128)S(1)} %copy-done.3, s32[2,1,128]{2,1,0:T(1,128)S(1)} %copy-done.4, s32[128]{0:T(128)S(1)} %copy-done.5, f32[15,128]{1,0:T(8,128)S(1)} %copy-done.1, f32[160,1440]{1,0:T(8,128)S(1)} %bitcast.1), custom_call_target="tpu_custom_call" | custom-call | tf_op jit(solution)/shard_map/transport/pallas_call | solution.py:454
  39.9 0.9 %copy.8 = f32[5,1,32,1440]{3,2,1,0:T(8,128)} copy(f32[5,1,32,1440]{3,2,1,0:T(8,128)S(1)} %transport.1) | data formatting | bytes 1843200
Async XLA Ops:
  0.0 0.7 %copy-start.5 = (s32[128]{0:T(128)S(1)}, s32[128]{0:T(128)}, u32[]{:S(2)}) copy-start(s32[128]{0:T(128)} %mask.1) | copy-start | bytes 1540
  0.0 0.7 %copy-start.2 = (f32[2,1,128]{2,1,0:T(1,128)S(1)}, f32[2,1,128]{2,1,0:T(1,128)}, u32[]{:S(2)}) copy-start(f32[2,1,128]{2,1,0:T(1,128)} %cx.1) | copy-start | bytes 3076
  0.7 1.2 %copy-start = (f32[5,1,32,1440]{3,2,1,0:T(8,128)S(1)}, f32[5,1,32,1440]{3,2,1,0:T(8,128)}, u32[]{:S(2)}) copy-start(f32[5,1,32,1440]{3,2,1,0:T(8,128)} %param.6) | copy-start | bytes 2764804
  1.9 0.7 %copy-start.1 = (f32[15,128]{1,0:T(8,128)S(1)}, f32[15,128]{1,0:T(8,128)}, u32[]{:S(2)}) copy-start(f32[15,128]{1,0:T(8,128)} %constant.2.clone.table) | copy-start | bytes 23044
  2.6 0.7 %copy-start.3 = (f32[2,1,128]{2,1,0:T(1,128)S(1)}, f32[2,1,128]{2,1,0:T(1,128)}, u32[]{:S(2)}) copy-start(f32[2,1,128]{2,1,0:T(1,128)} %cy.1) | copy-start | bytes 3076
  3.3 0.7 %copy-start.4 = (s32[2,1,128]{2,1,0:T(1,128)S(1)}, s32[2,1,128]{2,1,0:T(1,128)}, u32[]{:S(2)}) copy-start(s32[2,1,128]{2,1,0:T(1,128)} %shift.1) | copy-start | bytes 3076

commit v4 on v3

--- a/solution.py
+++ b/solution.py
@@ -13,7 +13,7 @@
 LANES = 128
 HALO = 2
 MESH = pl.DeviceIdType.MESH
-VMEM_LIMIT = 48 * 1024 * 1024
+VMEM_LIMIT = 62 * 1024 * 1024
 
 
 class Plan:
@@ -177,11 +177,13 @@
 
 
 def kernel(
-    plan, cx, cy, shift, mask, table, x_ref, out_ref,
-    packed, arrived, held, weights, ready, got, got_south, coef,
+    plan, *refs,
+):
+    inputs, (x_ref, out_ref), tables, rest = refs[:5], refs[5:7], refs[7:12], refs[12:]
+    cx, cy, shift, mask, table = tables
+    (x_local, x_sem, table_sem, packed, arrived, held, weights, ready, got, got_south, coef,
     in_send, in_recv, halo_send, halo_recv, south_in_send, south_in_recv,
-    out_send, out_recv, own_out, south_out_send, south_out_recv, own_in,
-):
+    out_send, out_recv, own_out, south_out_send, south_out_recv, own_in) = rest
     blocks, pitch, own, cols, lat = plan.blocks, plan.pitch, plan.own, plan.cols, plan.lat
     group, groups, slots = plan.group, plan.groups, plan.slots
     me = lax.axis_index("lon")
@@ -189,21 +191,54 @@
     has_north = band < plan.bands - 1
     north = lax.rem(band + 1, plan.bands)
 
+    has_south = band > 0
+    barrier = pltpu.get_barrier_semaphore()
+    for k in range(1, blocks):
+        pl.semaphore_signal(
+            barrier,
+            inc=1,
+            device_id={"lon": lax.rem(me + k, blocks), "lat": band},
+            device_id_type=MESH,
+        )
+    for there, to in ((has_north, north), (has_south, lax.rem(band + plan.bands - 1, plan.bands))):
+
+        @pl.when(there)
+        def _():
+            for k in range(blocks):
+                pl.semaphore_signal(
+                    barrier, inc=1, device_id={"lon": jnp.int32(k), "lat": to}, device_id_type=MESH
+                )
+
     def lines(first, count):
         return pl.ds(pl.multiple_of(first * pitch, 8), count * pitch)
 
+    def load(f):
+        part = pl.ds(f * lat, lat)
+        return pltpu.make_async_copy(x_ref.at[part], x_local.at[part], x_sem.at[f])
+
+    start_all([load(f) for f in range(plan.fields)])
+    table_copies = [
+        pltpu.make_async_copy(source, to, table_sem.at[i])
+        for i, (source, to) in enumerate(zip(inputs, tables))
+    ]
+    start_all(table_copies)
     packed[0 : HALO * pitch, :] = jnp.zeros((HALO * pitch, LANES), jnp.float32)
 
     def fill(part, none):
         for c in range(cols):
             width = LANES if c < cols - 1 else plan.rem
-            v = x_ref[pl.ds(pl.multiple_of(part * 8, 8), 8), c * LANES : c * LANES + width]
+            v = x_local[pl.ds(pl.multiple_of(part * 8, 8), 8), c * LANES : c * LANES + width]
             if width < LANES:
                 v = jnp.concatenate([v, jnp.zeros((8, LANES - width), jnp.float32)], axis=1)
             packed[pl.ds((part * 8 + HALO) * pitch + c, 8, stride=pitch), :] = v
         return none
 
-    lax.fori_loop(0, plan.rows // 8, fill, 0)
+    for f in range(plan.fields):
+        load(f).wait()
+        lax.fori_loop(f * (lat // 8), (f + 1) * (lat // 8), fill, 0)
+
+    bands_met = jnp.where(has_north, 1, 0) + jnp.where(has_south, 1, 0)
+    pl.semaphore_wait(barrier, blocks - 1 + blocks * bands_met)
 
     def peer(k):
         return lax.rem(me + k, blocks)
@@ -251,6 +286,9 @@
 
     for g in range(groups):
         start_all([group_in(k, g) for k in range(1, blocks)])
+
+    for copy in table_copies:
+        copy.wait()
 
     def place(slot):
         flat = me * own + slot - HALO
@@ -444,19 +482,24 @@
 def body(plan, fields, frac_x, frac_y, shift_cells, polar_mask):
     blocks, pitch, own, lat = plan.blocks, plan.pitch, plan.own, plan.lat
     vmem = pl.BlockSpec(memory_space=pltpu.VMEM)
-    smem = pl.BlockSpec(memory_space=pltpu.SMEM)
+    anywhere = pl.BlockSpec(memory_space=pltpu.HBM)
     dma = pltpu.SemaphoreType.DMA
     n_pieces = plan.fields * (HALO // plan.unit)
 
     def lines(rows):
         return pltpu.VMEM((rows * pitch, LANES), jnp.float32)
 
+    tables = (frac_x, frac_y, shift_cells, polar_mask, jnp.asarray(decay_table(plan)))
     return pl.pallas_call(
         functools.partial(kernel, plan),
         out_shape=jax.ShapeDtypeStruct(fields.shape, jnp.float32),
-        in_specs=[smem] * 5 + [vmem],
+        in_specs=[anywhere] * 6,
         out_specs=vmem,
         scratch_shapes=[
+            *[pltpu.SMEM(table.shape, table.dtype) for table in tables],
+            pltpu.VMEM((plan.rows, plan.lon), jnp.float32),
+            dma((plan.fields,)),
+            dma((len(tables),)),
             lines(HALO + plan.rows),
             lines(blocks * plan.slots),
             pltpu.VMEM((plan.slots, blocks, plan.cols * LANES), jnp.float32),
@@ -478,14 +521,12 @@
             dma((n_pieces,)),
             dma,
         ],
-        compiler_params=pltpu.CompilerParams(has_side_effects=True, vmem_limit_bytes=VMEM_LIMIT),
+        compiler_params=pltpu.CompilerParams(
+            collective_id=0, has_side_effects=True, vmem_limit_bytes=VMEM_LIMIT
+        ),
         name="transport",
     )(
-        frac_x,
-        frac_y,
-        shift_cells,
-        polar_mask,
-        jnp.asarray(decay_table(plan)),
+        *tables,
         fields.reshape(plan.rows, plan.lon),
     )
 

time: 41.1 us -> 35 us (0.85)
  Pallas kernels: 35.9 us -> 32.6 us
  local copies, waits for them, and re-layouts: 4.89 us -> 2.23 us
    pallas_call x1, Pallas kernels: 35.9 us -> 32.6 us  [body(): pl.pallas_call(functools.partial(kernel, plan), out_shape=jax.ShapeDtypeS...]
    unnamed x13 -> x1, local copies, waits for them, and re-layouts: 4.89 us -> 2.23 us
where the time goes in v4:
time: 35 us; the launch traced here: 34.8 us
  Pallas kernels  32.6 us (93%)
  local copies, waits for them, and re-layouts  2.23 us (6%)
    pallas_call x1, Pallas kernels, body(): pl.pallas_call(functools.partial(kernel, plan), out_shape=jax.ShapeDtypeS...  32.6 us
    unnamed x1, local copies, waits for them, and re-layouts  2.23 us

profile of v4, /device:TPU:9, one launch (start us, length us, event | category | flops | bytes accessed | tf_op | source)
XLA Modules:
  0.0 34.8 jit_solution(6086642993194523720)
XLA Ops:
  0.0 32.6 %transport.1 = f32[5,1,32,1440]{3,2,1,0:T(8,128)} custom-call(f32[2,1,128]{2,1,0:T(1,128)} %refs_0_.1, f32[2,1,128]{2,1,0:T(1,128)} %refs_1_.1, s32[2,1,128]{2,1,0:T(1,128)} %refs_2_.1, s32[128]{0:T(128)} %refs_3_.1, f32[15,128]{1,0:T(8,128)} %constant.2.clone.refs_4_, f32[160,1440]{1,0:T(8,128)} %bitcast.1), custom_call_target="tpu_custom_call" | custom-call | tf_op jit(solution)/shard_map/transport/pallas_call | solution.py:493
  32.6 2.2 %copy.8 = f32[5,1,32,1440]{3,2,1,0:T(8,128)} copy(f32[5,1,32,1440]{3,2,1,0:T(8,128)} %transport.1) | data formatting | bytes 1843200
